TPU v7x, 512 devices: a whole 4x8x8 slice. The times are simulated.
512 devices in a mesh: dom: 16 (over x_lo, y), gx: 4 (over x_hi, core), gy: 8 (over z).
Axes of the slice: x: 4 (x_hi: 2, x_lo: 2; x = x_hi * 2 + x_lo), y: 8, z: 8, core: 2. Of those that a mesh axis runs over, the one named last changes fastest.
Arguments:
- ensemble: float32 [16, 4, 32, 32, 1024], P('dom', None, None, 'gx', 'gy'), may hold values from -6 to 6
- ancestors: int32 [16, 4, 128], P(None, 'gx', 'gy'), may hold values from 0 to 15
- particle_air_drag: float32 [16, 2, 32, 1024], P('dom', None, 'gx', 'gy'), may hold values from -6 to 6
- eddy_diffusivity: float32 [31], replicated, may hold values from 0.02 to 0.15
Outputs:
- forecast: float32 [16, 4, 32, 32, 1024], P('dom', None, None, 'gx', 'gy')
All inputs are finite; a program needn't handle non-finite values.
Results may differ from a plain program's by a relative error of at most 0.0003.
Values sent between devices are 32-bit elements; how exact they have to be, the bound alone decides.
No kernel may reach another device: no remote copies, remote signals or barrier semaphores. Data moves between devices by JAX's collectives and lax.ppermute only.
A program may use at most 64 MiB of HBM per device.

v0:
```python
import jax
import jax.numpy as jnp
from jax import lax
from jax.sharding import PartitionSpec as P

STEPS = 4
TILE = 8


ADVECT = 0.2
DIFFUSE = 0.15
BUOY_TEMP = 0.2
BUOY_SALT = 0.1
PRESS_SCALE = 0.25
WIND_SCALE = 0.2
CORIO_BASE = 0.1
CORIO_SLOPE = 0.1


def extended(x, sides, width, wrap):
    for axis, dim in sides:
        size, length = (lax.axis_size(axis), x.shape[dim])
        up = [(i, (i + 1) % size) for i in range(size if wrap else size - 1)]
        down = [(j, i) for i, j in up]
        last = lax.slice_in_dim(x, length - width, length, axis=dim)
        leading = lax.slice_in_dim(x, 0, width, axis=dim)
        before = lax.ppermute(last, axis, up)
        after = lax.ppermute(leading, axis, down)
        x = jnp.concatenate([before, x, after], axis=dim)
    return x


def advance(padded, topmost_slab, eddy_diffusivity, coriolis):
    centre = padded[:, :, 1:-1, 1:-1]
    eastern_neighbour_cell = padded[:, :, 2:, 1:-1]
    west_cell = padded[:, :, :-2, 1:-1]
    north_cell = padded[:, :, 1:-1, 2:]
    south_cell = padded[:, :, 1:-1, :-2]
    grad_x = 0.5 * (eastern_neighbour_cell - west_cell)
    grad_y = 0.5 * (north_cell - south_cell)
    spread = eastern_neighbour_cell + west_cell + north_cell + south_cell - 4.0 * centre
    buoyancy = BUOY_TEMP * padded[2] - BUOY_SALT * padded[3]
    pressure = PRESS_SCALE * jnp.cumsum(buoyancy, axis=0)
    press_x = 0.5 * (pressure[:, 2:, 1:-1] - pressure[:, :-2, 1:-1])
    press_y = 0.5 * (pressure[:, 1:-1, 2:] - pressure[:, 1:-1, :-2])
    vert_flux = eddy_diffusivity[None, :, None, None] * (centre[:, 1:] - centre[:, :-1])
    closed = jnp.zeros_like(centre[:, :1])
    vertical = jnp.concatenate([vert_flux, closed], axis=1) - jnp.concatenate(
        [closed, vert_flux], axis=1
    )
    east_vel = centre[0]
    north_vel = centre[1]
    carried_over = east_vel[None] * grad_x + north_vel[None] * grad_y
    common = centre - ADVECT * carried_over + DIFFUSE * spread + vertical
    level_top = (jnp.arange(centre.shape[1]) == 0).astype(jnp.float32)[:, None, None]
    forcing = WIND_SCALE * topmost_slab[:, None] * level_top
    east_next = common[0] + coriolis * north_vel - press_x + forcing[0]
    north_next = common[1] - coriolis * east_vel - press_y + forcing[1]
    return jnp.stack([east_next, north_next, common[2], common[3]])


def coriolis_at(positions, total_rows):
    return CORIO_BASE + CORIO_SLOPE * (positions.astype(jnp.float32) + 0.5) / total_rows


def per_device(ensemble, ancestors, particle_air_drag, eddy_diffusivity):
    particle_number = lax.axis_index("dom")
    width_y = ensemble.shape[4]
    own_tiles = lax.dynamic_index_in_dim(ancestors, particle_number, 0, keepdims=False)
    cell_source = jnp.repeat(jnp.repeat(own_tiles, TILE, 0), TILE, 1)
    shards = lax.all_gather(ensemble, "dom", axis=0, tiled=True)

    def place(offset, partial_state):
        wanted = (cell_source == offset)[None, None]
        return jnp.where(wanted, shards[offset], partial_state)

    selected_particles = lax.fori_loop(
        0, shards.shape[0], place, jnp.zeros(ensemble.shape[1:], jnp.float32)
    )
    row_block = lax.axis_index("gy")
    total_rows = width_y * lax.axis_size("gy")
    topmost_slab = particle_air_drag[0]
    positions = row_block * width_y + jnp.arange(width_y, dtype=jnp.int32)
    coriolis = coriolis_at(positions, total_rows)
    marine_variables = selected_particles
    for iteration in range(STEPS):
        widened = extended(marine_variables, (("gx", 2),), 1, True)
        padded = extended(widened, (("gy", 3),), 1, False)
        marine_variables = advance(padded, topmost_slab, eddy_diffusivity, coriolis)
    return marine_variables[None]


def solution(mesh):
    placed = (
        P("dom", None, None, "gx", "gy"),
        P(None, "gx", "gy"),
        P("dom", None, "gx", "gy"),
        P(),
    )
    return jax.shard_map(
        per_device,
        mesh=mesh,
        in_specs=placed,
        out_specs=P("dom", None, None, "gx", "gy"),
        check_vma=False,
    )
```

profile of v0, /device:TPU:192, one launch (start us, length us, event | category | flops | bytes accessed | tf_op | source)
XLA Modules:
  0.0 242.2 jit_solution(3216205016897837042)
XLA Ops:
  8.3 106.9 %all-gather.2.cloned.1.call-done = f32[16,4,32,8,128]{4,3,2,1,0:T(8,128)} async-done(((f32[1,4,32,8,128]{4,3,2,1,0:T(8,128)}), f32[16,4,32,8,128]{4,3,2,1,0:T(8,128)}) %all-gather.2.cloned.1.call-update) | async-done | bytes 8388624 | tf_op jit(solution)/shard_map/all_gather | solution.py:71
  115.2 19.9 %while.14 = (s32[]{:T(128)}, f32[4,32,8,128]{3,2,1,0:T(8,128)S(1)}, f32[16,4,32,8,128]{4,3,2,1,0:T(8,128)}, s32[128]{0:T(128)S(1)}, s32[]{:T(128)}, /*index=5*/s32[]{:T(128)}) while((s32[]{:T(128)}, f32[4,32,8,128]{3,2,1,0:T(8,128)S(1)}, f32[16,4,32,8,128]{4,3,2,1,0:T(8,128)}, s32[128]{0:T(128)S(1)}, s32[]{:T(128)}, ...), condition=%wide.region_1.2_spmd.clone, body=%wide.region_0.1_spmd.clone.sunk | while | flops 262275 | bytes 1573719 | solution.py:77
  117.7 1.2 bitcast_select_fusion.2
  120.2 1.2 bitcast_select_fusion.2
  135.2 3.9 %collective-permute-start = (f32[4,32,1,128]{3,2,1,0:T(1,128)S(1)}, f32[4,32,1,128]{3,2,1,0:T(1,128)S(1)}, u32[]{:S(2)}, u32[]{:S(2)}) collective-permute-start(f32[4,32,1,128]{3,2,1,0:T(1,128)S(1)} %get-tuple-element.148), channel_id=1, source_target_pairs={{8,0},{16,8},{24,16},{0,24},{9,1},{17,9},{25,17},{1,25},{10,2},{18... | collective-permute-start | bytes 196616 | tf_op jit(solution)/shard_map/ppermute | solution.py:28
  139.1 1.9 collective-permute-start.1
  141.9 4.3 %collective-permute-done.1 = f32[4,32,1,128]{3,2,1,0:T(1,128)S(1)} collective-permute-done((f32[4,32,1,128]{3,2,1,0:T(1,128)S(1)}, f32[4,32,1,128]{3,2,1,0:T(1,128)S(1)}, u32[]{:S(2)}, u32[]{:S(2)}) %collective-permute-start.1) | collective-permute-done | bytes 65568 | tf_op jit(solution)/shard_map/ppermute | solution.py:27
  147.1 2.3 collective-permute-start.2
  149.8 4.8 %collective-permute-start.3 = (f32[4,32,10,1]{1,0,3,2:T(4,128)S(1)}, f32[4,32,10,1]{1,0,3,2:T(4,128)S(1)}, u32[]{:S(2)}, u32[]{:S(2)}) collective-permute-start(f32[4,32,10,1]{1,0,3,2:T(4,128)S(1)} %copy.7), channel_id=1, source_target_pairs={{0,1},{1,2},{2,3},{3,4},{4,5},{5,6},{6,7},{8,9},{9,10},{10,11},{11... | collective-permute-start | bytes 15368 | tf_op jit(solution)/shard_map/ppermute | solution.py:27
  156.5 2.2 subtract_add_fusion.3
  160.5 1.9 collective-permute-start.4
  162.4 2.4 collective-permute-start.5
  164.9 4.7 %collective-permute-done.5 = f32[4,32,1,128]{3,2,1,0:T(1,128)S(1)} collective-permute-done((f32[4,32,1,128]{3,2,1,0:T(1,128)S(1)}, f32[4,32,1,128]{3,2,1,0:T(1,128)S(1)}, u32[]{:S(2)}, u32[]{:S(2)}) %collective-permute-start.5) | collective-permute-done | bytes 65568 | tf_op jit(solution)/shard_map/ppermute | solution.py:27
  171.1 1.9 collective-permute-start.6
  173.4 5.4 %collective-permute-start.7 = (f32[4,32,10,1]{1,0,3,2:T(4,128)S(1)}, f32[4,32,10,1]{1,0,3,2:T(4,128)}, u32[]{:S(2)}, u32[]{:S(2)}) collective-permute-start(f32[4,32,10,1]{1,0,3,2:T(4,128)S(1)} %copy.13), channel_id=1, source_target_pairs={{0,1},{1,2},{2,3},{3,4},{4,5},{5,6},{6,7},{8,9},{9,10},{10,11},{11... | collective-permute-start | bytes 15368 | tf_op jit(solution)/shard_map/ppermute | solution.py:27
  180.3 1.2 copy.14
  181.5 2.2 subtract_add_fusion.2
  184.8 1.9 collective-permute-start.8
  186.8 2.4 collective-permute-start.9
  189.2 4.7 %collective-permute-done.9 = f32[4,32,1,128]{3,2,1,0:T(1,128)S(1)} collective-permute-done((f32[4,32,1,128]{3,2,1,0:T(1,128)S(1)}, f32[4,32,1,128]{3,2,1,0:T(1,128)S(1)}, u32[]{:S(2)}, u32[]{:S(2)}) %collective-permute-start.9) | collective-permute-done | bytes 65568 | tf_op jit(solution)/shard_map/ppermute | solution.py:27
  194.0 1.3 fusion.130
  195.4 1.6 copy.17
  196.9 1.9 collective-permute-start.10
  199.3 5.7 %collective-permute-start.11 = (f32[4,32,10,1]{1,0,3,2:T(4,128)S(1)}, f32[4,32,10,1]{1,0,3,2:T(4,128)S(1)}, u32[]{:S(2)}, u32[]{:S(2)}) collective-permute-start(f32[4,32,10,1]{1,0,3,2:T(4,128)S(1)} %copy.19), channel_id=1, source_target_pairs={{0,1},{1,2},{2,3},{3,4},{4,5},{5,6},{6,7},{8,9},{9,10},{10,11},{11... | collective-permute-start | bytes 15368 | tf_op jit(solution)/shard_map/ppermute | solution.py:27
  206.9 2.1 subtract_add_fusion.1
  210.9 1.9 collective-permute-start.12
  212.8 2.4 collective-permute-start.13
  215.2 4.7 %collective-permute-done.13 = f32[4,32,1,128]{3,2,1,0:T(1,128)S(1)} collective-permute-done((f32[4,32,1,128]{3,2,1,0:T(1,128)S(1)}, f32[4,32,1,128]{3,2,1,0:T(1,128)S(1)}, u32[]{:S(2)}, u32[]{:S(2)}) %collective-permute-start.13) | collective-permute-done | bytes 65568 | tf_op jit(solution)/shard_map/ppermute | solution.py:27
  221.4 1.9 collective-permute-start.14
  223.8 5.2 %collective-permute-start.15 = (f32[4,32,10,1]{1,0,3,2:T(4,128)S(1)}, f32[4,32,10,1]{1,0,3,2:T(4,128)}, u32[]{:S(2)}, u32[]{:S(2)}) collective-permute-start(f32[4,32,10,1]{1,0,3,2:T(4,128)S(1)} %copy.25), channel_id=1, source_target_pairs={{0,1},{1,2},{2,3},{3,4},{4,5},{5,6},{6,7},{8,9},{9,10},{10,11},{11... | collective-permute-start | bytes 15368 | tf_op jit(solution)/shard_map/ppermute | solution.py:27
  230.5 1.2 copy.26
  231.7 1.8 subtract_add_fusion
  (101 shorter events, 38.7 us)
Async XLA Ops:
  6.5 0.7 copy-start
  6.5 134.5 %copy-start.1 = (f32[31]{0:T(128)S(1)}, f32[31]{0:T(128)}, u32[]{:S(2)}) copy-start(f32[31]{0:T(128)} %param.9) | copy-start | bytes 376
  6.5 108.6 %all-gather.2.cloned.1.call-start = ((), (), s32[]{:S(2)}) async-start(), calls=%async_computation | async-start | bytes 8912896 | tf_op jit(solution)/shard_map/all_gather | solution.py:71
  135.2 6.7 %collective-permute-start = (f32[4,32,1,128]{3,2,1,0:T(1,128)S(1)}, f32[4,32,1,128]{3,2,1,0:T(1,128)S(1)}, u32[]{:S(2)}, u32[]{:S(2)}) collective-permute-start(f32[4,32,1,128]{3,2,1,0:T(1,128)S(1)} %get-tuple-element.148), channel_id=1, source_target_pairs={{8,0},{16,8},{24,16},{0,24},{9,1},{17,9},{25,17},{1,25},{10,2},{18... | collective-permute-start | bytes 196616 | tf_op jit(solution)/shard_map/ppermute | solution.py:28
  139.1 7.1 %collective-permute-start.1 = (f32[4,32,1,128]{3,2,1,0:T(1,128)S(1)}, f32[4,32,1,128]{3,2,1,0:T(1,128)S(1)}, u32[]{:S(2)}, u32[]{:S(2)}) collective-permute-start(f32[4,32,1,128]{3,2,1,0:T(1,128)S(1)} %get-tuple-element.147), channel_id=1, source_target_pairs={{0,8},{8,16},{16,24},{24,0},{1,9},{9,17},{17,25},{25,1},{2,10},{10... | collective-permute-start | bytes 196616 | tf_op jit(solution)/shard_map/ppermute | solution.py:27
  147.1 7.5 %collective-permute-start.2 = (f32[4,32,10,1]{1,0,3,2:T(4,128)S(1)}, f32[4,32,10,1]{1,0,3,2:T(4,128)S(1)}, u32[]{:S(2)}, u32[]{:S(2)}) collective-permute-start(f32[4,32,10,1]{1,0,3,2:T(4,128)S(1)} %copy.5), channel_id=1, source_target_pairs={{1,0},{2,1},{3,2},{4,3},{5,4},{6,5},{7,6},{9,8},{10,9},{11,10},{12... | collective-permute-start | bytes 15368 | tf_op jit(solution)/shard_map/ppermute | solution.py:28
  149.8 6.2 %collective-permute-start.3 = (f32[4,32,10,1]{1,0,3,2:T(4,128)S(1)}, f32[4,32,10,1]{1,0,3,2:T(4,128)S(1)}, u32[]{:S(2)}, u32[]{:S(2)}) collective-permute-start(f32[4,32,10,1]{1,0,3,2:T(4,128)S(1)} %copy.7), channel_id=1, source_target_pairs={{0,1},{1,2},{2,3},{3,4},{4,5},{5,6},{6,7},{8,9},{9,10},{10,11},{11... | collective-permute-start | bytes 15368 | tf_op jit(solution)/shard_map/ppermute | solution.py:27
  160.5 4.3 %collective-permute-start.4 = (f32[4,32,1,128]{3,2,1,0:T(1,128)S(1)}, f32[4,32,1,128]{3,2,1,0:T(1,128)S(1)}, u32[]{:S(2)}, u32[]{:S(2)}) collective-permute-start(f32[4,32,1,128]{3,2,1,0:T(1,128)S(1)} %get-tuple-element.144), channel_id=1, source_target_pairs={{8,0},{16,8},{24,16},{0,24},{9,1},{17,9},{25,17},{1,25},{10,2},{18... | collective-permute-start | bytes 196616 | tf_op jit(solution)/shard_map/ppermute | solution.py:28
  162.4 7.1 %collective-permute-start.5 = (f32[4,32,1,128]{3,2,1,0:T(1,128)S(1)}, f32[4,32,1,128]{3,2,1,0:T(1,128)S(1)}, u32[]{:S(2)}, u32[]{:S(2)}) collective-permute-start(f32[4,32,1,128]{3,2,1,0:T(1,128)S(1)} %get-tuple-element.143), channel_id=1, source_target_pairs={{0,8},{8,16},{16,24},{24,0},{1,9},{9,17},{17,25},{25,1},{2,10},{10... | collective-permute-start | bytes 196616 | tf_op jit(solution)/shard_map/ppermute | solution.py:27
  171.1 8.6 %collective-permute-start.6 = (f32[4,32,10,1]{1,0,3,2:T(4,128)}, f32[4,32,10,1]{1,0,3,2:T(4,128)S(1)}, u32[]{:S(2)}, u32[]{:S(2)}) collective-permute-start(f32[4,32,10,1]{1,0,3,2:T(4,128)} %copy.11), channel_id=1, source_target_pairs={{1,0},{2,1},{3,2},{4,3},{5,4},{6,5},{7,6},{9,8},{10,9},{11,10},{12... | collective-permute-start | bytes 15368 | tf_op jit(solution)/shard_map/ppermute | solution.py:28
  173.4 6.9 %collective-permute-start.7 = (f32[4,32,10,1]{1,0,3,2:T(4,128)S(1)}, f32[4,32,10,1]{1,0,3,2:T(4,128)}, u32[]{:S(2)}, u32[]{:S(2)}) collective-permute-start(f32[4,32,10,1]{1,0,3,2:T(4,128)S(1)} %copy.13), channel_id=1, source_target_pairs={{0,1},{1,2},{2,3},{3,4},{4,5},{5,6},{6,7},{8,9},{9,10},{10,11},{11... | collective-permute-start | bytes 15368 | tf_op jit(solution)/shard_map/ppermute | solution.py:27
  184.8 4.3 %collective-permute-start.8 = (f32[4,32,1,128]{3,2,1,0:T(1,128)S(1)}, f32[4,32,1,128]{3,2,1,0:T(1,128)S(1)}, u32[]{:S(2)}, u32[]{:S(2)}) collective-permute-start(f32[4,32,1,128]{3,2,1,0:T(1,128)S(1)} %get-tuple-element.142), channel_id=1, source_target_pairs={{8,0},{16,8},{24,16},{0,24},{9,1},{17,9},{25,17},{1,25},{10,2},{18... | collective-permute-start | bytes 196616 | tf_op jit(solution)/shard_map/ppermute | solution.py:28
  186.8 7.1 %collective-permute-start.9 = (f32[4,32,1,128]{3,2,1,0:T(1,128)S(1)}, f32[4,32,1,128]{3,2,1,0:T(1,128)S(1)}, u32[]{:S(2)}, u32[]{:S(2)}) collective-permute-start(f32[4,32,1,128]{3,2,1,0:T(1,128)S(1)} %get-tuple-element.141), channel_id=1, source_target_pairs={{0,8},{8,16},{16,24},{24,0},{1,9},{9,17},{17,25},{25,1},{2,10},{10... | collective-permute-start | bytes 196616 | tf_op jit(solution)/shard_map/ppermute | solution.py:27
  196.9 8.9 %collective-permute-start.10 = (f32[4,32,10,1]{1,0,3,2:T(4,128)S(1)}, f32[4,32,10,1]{1,0,3,2:T(4,128)S(1)}, u32[]{:S(2)}, u32[]{:S(2)}) collective-permute-start(f32[4,32,10,1]{1,0,3,2:T(4,128)S(1)} %copy.17), channel_id=1, source_target_pairs={{1,0},{2,1},{3,2},{4,3},{5,4},{6,5},{7,6},{9,8},{10,9},{11,10},{12... | collective-permute-start | bytes 15368 | tf_op jit(solution)/shard_map/ppermute | solution.py:28
  199.3 7.1 %collective-permute-start.11 = (f32[4,32,10,1]{1,0,3,2:T(4,128)S(1)}, f32[4,32,10,1]{1,0,3,2:T(4,128)S(1)}, u32[]{:S(2)}, u32[]{:S(2)}) collective-permute-start(f32[4,32,10,1]{1,0,3,2:T(4,128)S(1)} %copy.19), channel_id=1, source_target_pairs={{0,1},{1,2},{2,3},{3,4},{4,5},{5,6},{6,7},{8,9},{9,10},{10,11},{11... | collective-permute-start | bytes 15368 | tf_op jit(solution)/shard_map/ppermute | solution.py:27
  210.9 4.3 %collective-permute-start.12 = (f32[4,32,1,128]{3,2,1,0:T(1,128)S(1)}, f32[4,32,1,128]{3,2,1,0:T(1,128)S(1)}, u32[]{:S(2)}, u32[]{:S(2)}) collective-permute-start(f32[4,32,1,128]{3,2,1,0:T(1,128)S(1)} %get-tuple-element.140), channel_id=1, source_target_pairs={{8,0},{16,8},{24,16},{0,24},{9,1},{17,9},{25,17},{1,25},{10,2},{18... | collective-permute-start | bytes 196616 | tf_op jit(solution)/shard_map/ppermute | solution.py:28
  212.8 7.1 %collective-permute-start.13 = (f32[4,32,1,128]{3,2,1,0:T(1,128)S(1)}, f32[4,32,1,128]{3,2,1,0:T(1,128)S(1)}, u32[]{:S(2)}, u32[]{:S(2)}) collective-permute-start(f32[4,32,1,128]{3,2,1,0:T(1,128)S(1)} %get-tuple-element.139), channel_id=1, source_target_pairs={{0,8},{8,16},{16,24},{24,0},{1,9},{9,17},{17,25},{25,1},{2,10},{10... | collective-permute-start | bytes 196616 | tf_op jit(solution)/shard_map/ppermute | solution.py:27
  221.4 7.7 %collective-permute-start.14 = (f32[4,32,10,1]{1,0,3,2:T(4,128)}, f32[4,32,10,1]{1,0,3,2:T(4,128)S(1)}, u32[]{:S(2)}, u32[]{:S(2)}) collective-permute-start(f32[4,32,10,1]{1,0,3,2:T(4,128)} %copy.23), channel_id=1, source_target_pairs={{1,0},{2,1},{3,2},{4,3},{5,4},{6,5},{7,6},{9,8},{10,9},{11,10},{12... | collective-permute-start | bytes 15368 | tf_op jit(solution)/shard_map/ppermute | solution.py:28
  223.8 6.7 %collective-permute-start.15 = (f32[4,32,10,1]{1,0,3,2:T(4,128)S(1)}, f32[4,32,10,1]{1,0,3,2:T(4,128)}, u32[]{:S(2)}, u32[]{:S(2)}) collective-permute-start(f32[4,32,10,1]{1,0,3,2:T(4,128)S(1)} %copy.25), channel_id=1, source_target_pairs={{0,1},{1,2},{2,3},{3,4},{4,5},{5,6},{6,7},{8,9},{9,10},{10,11},{11... | collective-permute-start | bytes 15368 | tf_op jit(solution)/shard_map/ppermute | solution.py:27
Sparse Core Ops, SparseCore 0:
  9.4 105.7 all-gather.1
where the time goes:
time: 244 us; the launch traced here: 242 us
  waiting for transfers between devices  128 us (52%)
  starting transfers between devices  47.9 us (20%)
  other arithmetic  38.3 us (16%)
  local copies, waits for them, and re-layouts  14.2 us (6%)
  between operations  13.9 us (6%)
    all_gather x1, waiting for transfers between devices, per_device(): shards = lax.all_gather(ensemble, 'dom', axis=0, tiled=True)  107 us
    ppermute x8, starting transfers between devices, extended(): before = lax.ppermute(last, axis, up)  30.2 us
    ppermute x8, waiting for transfers between devices, extended(): before = lax.ppermute(last, axis, up)  20 us
    select_n x16, other arithmetic, place(): return jnp.where(wanted, shards[offset], partial_state)  19.4 us
    ppermute x8, starting transfers between devices, extended(): after = lax.ppermute(leading, axis, down)  17.6 us
    add x4, other arithmetic, advance(): common = centre - ADVECT * carried_over + DIFFUSE * spread + vertical  8.36 us
  transfers between devices with their start and end apart: 17, of which 7 were waited for; matrix products, arithmetic and copies ran while one was open for 3% of the time, Pallas kernels for 0%

commit v1 on v0

--- a/solution.py
+++ b/solution.py
@@ -63,20 +63,25 @@
     return CORIO_BASE + CORIO_SLOPE * (positions.astype(jnp.float32) + 0.5) / total_rows
 
 
+def resample(ensemble, ancestors):
+    members = lax.axis_size("dom")
+    block = ensemble[0]
+    fields, levels, width_x, width_y = block.shape
+    groups = fields * levels // members
+    parts = block.reshape(members, groups, width_x, width_y)
+    by_member = lax.all_to_all(parts, "dom", 0, 0, tiled=True)
+    tiles = ancestors[:, 0, :]
+    cell_source = jnp.repeat(tiles, TILE, 1)[:, None, None, :]
+    picked = jnp.zeros_like(by_member)
+    for member in range(members):
+        picked = jnp.where(cell_source == member, by_member[member][None], picked)
+    back = lax.all_to_all(picked, "dom", 0, 0, tiled=True)
+    return back.reshape(fields, levels, width_x, width_y)
+
+
 def per_device(ensemble, ancestors, particle_air_drag, eddy_diffusivity):
-    particle_number = lax.axis_index("dom")
     width_y = ensemble.shape[4]
-    own_tiles = lax.dynamic_index_in_dim(ancestors, particle_number, 0, keepdims=False)
-    cell_source = jnp.repeat(jnp.repeat(own_tiles, TILE, 0), TILE, 1)
-    shards = lax.all_gather(ensemble, "dom", axis=0, tiled=True)
-
-    def place(offset, partial_state):
-        wanted = (cell_source == offset)[None, None]
-        return jnp.where(wanted, shards[offset], partial_state)
-
-    selected_particles = lax.fori_loop(
-        0, shards.shape[0], place, jnp.zeros(ensemble.shape[1:], jnp.float32)
-    )
+    selected_particles = resample(ensemble, ancestors)
     row_block = lax.axis_index("gy")
     total_rows = width_y * lax.axis_size("gy")
     topmost_slab = particle_air_drag[0]

time: 244 us -> 149 us (0.61)
  the two profiles are of different devices: /device:TPU:192 before, /device:TPU:200 now
where the time goes in v1:
time: 149 us; the launch traced here: 147 us
  starting transfers between devices  61.6 us (41%)
  waiting for transfers between devices  46.3 us (31%)
  local copies, waits for them, and re-layouts  19.9 us (13%)
  other arithmetic  19.1 us (13%)
    ppermute x8, starting transfers between devices, extended(): before = lax.ppermute(last, axis, up)  31.1 us
    ppermute x8, waiting for transfers between devices, extended(): before = lax.ppermute(last, axis, up)  20.7 us
    ppermute x8, starting transfers between devices, extended(): after = lax.ppermute(leading, axis, down)  16.6 us
    all_to_all x1, waiting for transfers between devices, resample(): back = lax.all_to_all(picked, 'dom', 0, 0, tiled=True)  13.9 us
    all_to_all x1, waiting for transfers between devices, resample(): by_member = lax.all_to_all(parts, 'dom', 0, 0, tiled=True)  11.7 us
    all_to_all x1, starting transfers between devices, resample(): by_member = lax.all_to_all(parts, 'dom', 0, 0, tiled=True)  8.62 us
    add x4, other arithmetic, advance(): common = centre - ADVECT * carried_over + DIFFUSE * spread + vertical  8.02 us
    slice x12, local copies, waits for them, and re-layouts, extended(): last = lax.slice_in_dim(x, length - width, length, axis=dim)  5.32 us
  transfers between devices with their start and end apart: 18, of which 8 were waited for; matrix products, arithmetic and copies ran while one was open for 6% of the time, Pallas kernels for 0%

profile of v1, /device:TPU:200, one launch (start us, length us, event | category | flops | bytes accessed | tf_op | source)
XLA Modules:
  0.0 147.4 jit_solution(3874169432731567196)
XLA Ops:
  0.0 8.6 %all-to-all-start = ((f32[16,8,8,128]{3,2,1,0:T(8,128)}), f32[16,8,8,128]{3,2,1,0:T(8,128)S(1)}, u32[]{:S(2)}, u32[]{:S(2)}) async-start(f32[16,8,8,128]{3,2,1,0:T(8,128)} %bitcast.229), calls=%async_computation | async-start | bytes 1048576 | tf_op jit(solution)/shard_map/all_to_all | solution.py:72
  11.9 11.7 %all-to-all-done = f32[16,8,8,128]{3,2,1,0:T(8,128)S(1)} async-done(((f32[16,8,8,128]{3,2,1,0:T(8,128)}), f32[16,8,8,128]{3,2,1,0:T(8,128)S(1)}, u32[]{:S(2)}, u32[]{:S(2)}) %all-to-all-start) | async-done | bytes 524320 | tf_op jit(solution)/shard_map/all_to_all | solution.py:72
  23.6 1.9 %select_select_fusion = f32[16,8,8,128]{3,2,1,0:T(8,128)} fusion(f32[8,8,128]{2,1,0:T(8,128)S(1)} %get-tuple-element.44, f32[8,8,128]{2,1,0:T(8,128)S(1)} %get-tuple-element.45, f32[8,8,128]{2,1,0:T(8,128)S(1)} %get-tuple-element.46, f32[8,8,128]{2,1,0:T(8,128)S(1)} %get-tuple-element.47, f32[8,8,128]{2,1,0:T(8,128)S(1)} %get-tuple-element.48, ...), kind=kLoop, calls=%fused_computation.158 | loop fusion | flops 2097152 | bytes 1081344 | tf_op jit(solution)/shard_map/jit(_where)/select_n | solution.py:77
  25.5 5.3 %all-to-all-start.1 = ((f32[16,8,8,128]{3,2,1,0:T(8,128)}), f32[16,8,8,128]{3,2,1,0:T(8,128)S(1)}, u32[]{:S(2)}, u32[]{:S(2)}) async-start(f32[16,8,8,128]{3,2,1,0:T(8,128)} %select_select_fusion), calls=%async_computation.1 | async-start | bytes 1048576 | tf_op jit(solution)/shard_map/all_to_all | solution.py:78
  31.6 13.9 %all-to-all-done.1 = f32[16,8,8,128]{3,2,1,0:T(8,128)S(1)} async-done(((f32[16,8,8,128]{3,2,1,0:T(8,128)}), f32[16,8,8,128]{3,2,1,0:T(8,128)S(1)}, u32[]{:S(2)}, u32[]{:S(2)}) %all-to-all-start.1) | async-done | bytes 524320 | tf_op jit(solution)/shard_map/all_to_all | solution.py:78
  47.1 3.2 %collective-permute-start = (f32[4,32,1,128]{3,2,1,0:T(1,128)S(1)}, f32[4,32,1,128]{3,2,1,0:T(1,128)S(1)}, u32[]{:S(2)}, u32[]{:S(2)}) collective-permute-start(f32[4,32,1,128]{3,2,1,0:T(1,128)S(1)} %get-tuple-element.42), channel_id=1, source_target_pairs={{8,0},{16,8},{24,16},{0,24},{9,1},{17,9},{25,17},{1,25},{10,2},{18... | collective-permute-start | bytes 196616 | tf_op jit(solution)/shard_map/ppermute | solution.py:28
  50.2 1.9 %collective-permute-start.1 = (f32[4,32,1,128]{3,2,1,0:T(1,128)S(1)}, f32[4,32,1,128]{3,2,1,0:T(1,128)S(1)}, u32[]{:S(2)}, u32[]{:S(2)}) collective-permute-start(f32[4,32,1,128]{3,2,1,0:T(1,128)S(1)} %get-tuple-element.41), channel_id=1, source_target_pairs={{0,8},{8,16},{16,24},{24,0},{1,9},{9,17},{17,25},{25,1},{2,10},{10... | collective-permute-start | bytes 196616 | tf_op jit(solution)/shard_map/ppermute | solution.py:27
  52.2 5.1 %collective-permute-done.1 = f32[4,32,1,128]{3,2,1,0:T(1,128)S(1)} collective-permute-done((f32[4,32,1,128]{3,2,1,0:T(1,128)S(1)}, f32[4,32,1,128]{3,2,1,0:T(1,128)S(1)}, u32[]{:S(2)}, u32[]{:S(2)}) %collective-permute-start.1) | collective-permute-done | bytes 65568 | tf_op jit(solution)/shard_map/ppermute | solution.py:27
  58.3 1.9 %collective-permute-start.2 = (f32[4,32,10,1]{1,0,3,2:T(4,128)S(1)}, f32[4,32,10,1]{1,0,3,2:T(4,128)S(1)}, u32[]{:S(2)}, u32[]{:S(2)}) collective-permute-start(f32[4,32,10,1]{1,0,3,2:T(4,128)S(1)} %copy.69), channel_id=1, source_target_pairs={{1,0},{2,1},{3,2},{4,3},{5,4},{6,5},{7,6},{9,8},{10,9},{11,10},{12... | collective-permute-start | bytes 15368 | tf_op jit(solution)/shard_map/ppermute | solution.py:28
  60.6 5.5 %collective-permute-start.3 = (f32[4,32,10,1]{1,0,3,2:T(4,128)S(1)}, f32[4,32,10,1]{1,0,3,2:T(4,128)}, u32[]{:S(2)}, u32[]{:S(2)}) collective-permute-start(f32[4,32,10,1]{1,0,3,2:T(4,128)S(1)} %copy.71), channel_id=1, source_target_pairs={{0,1},{1,2},{2,3},{3,4},{4,5},{5,6},{6,7},{8,9},{9,10},{10,11},{11... | collective-permute-start | bytes 15368 | tf_op jit(solution)/shard_map/ppermute | solution.py:27
  68.8 2.1 %subtract_add_fusion.3 = f32[4,32,8,128]{3,2,1,0:T(8,128)S(1)} fusion(f32[4,31,8,128]{3,2,1,0:T(8,128)} %fusion.67, f32[4,32,8,128]{3,2,1,0:T(8,128)S(1)} %bitcast.203, f32[4,32,10,1]{3,2,1,0:T(8,128)S(1)} %copy.70, f32[4,32,1,128]{3,2,1,0:T(1,128)S(1)} %collective-permute-done, f32[4,32,1,128]{3,2,1,0:T(1,128)S(1)} %collective-permute-done.1, ...), kind=kLoop, calls=%fused_computation.157 | loop fusion | flops 3145728 | bytes 1959936 | tf_op jit(solution)/shard_map/add | solution.py:54
  72.0 1.9 %collective-permute-start.4 = (f32[4,32,1,128]{3,2,1,0:T(1,128)S(1)}, f32[4,32,1,128]{3,2,1,0:T(1,128)S(1)}, u32[]{:S(2)}, u32[]{:S(2)}) collective-permute-start(f32[4,32,1,128]{3,2,1,0:T(1,128)S(1)} %get-tuple-element.38), channel_id=1, source_target_pairs={{8,0},{16,8},{24,16},{0,24},{9,1},{17,9},{25,17},{1,25},{10,2},{18... | collective-permute-start | bytes 196616 | tf_op jit(solution)/shard_map/ppermute | solution.py:28
  73.9 2.4 %collective-permute-start.5 = (f32[4,32,1,128]{3,2,1,0:T(1,128)S(1)}, f32[4,32,1,128]{3,2,1,0:T(1,128)S(1)}, u32[]{:S(2)}, u32[]{:S(2)}) collective-permute-start(f32[4,32,1,128]{3,2,1,0:T(1,128)S(1)} %get-tuple-element.37), channel_id=1, source_target_pairs={{0,8},{8,16},{16,24},{24,0},{1,9},{9,17},{17,25},{25,1},{2,10},{10... | collective-permute-start | bytes 196616 | tf_op jit(solution)/shard_map/ppermute | solution.py:27
  76.3 4.7 %collective-permute-done.5 = f32[4,32,1,128]{3,2,1,0:T(1,128)S(1)} collective-permute-done((f32[4,32,1,128]{3,2,1,0:T(1,128)S(1)}, f32[4,32,1,128]{3,2,1,0:T(1,128)S(1)}, u32[]{:S(2)}, u32[]{:S(2)}) %collective-permute-start.5) | collective-permute-done | bytes 65568 | tf_op jit(solution)/shard_map/ppermute | solution.py:27
  81.2 1.3 fusion.130
  82.5 1.6 %copy.75 = f32[4,32,10,1]{1,0,3,2:T(4,128)S(1)} copy(f32[4,32,10,1]{3,2,1,0:T(8,128)} %get-tuple-element.30) | data formatting | bytes 10240 | tf_op jit(solution)/shard_map/slice | solution.py:26
  84.1 1.9 %collective-permute-start.6 = (f32[4,32,10,1]{1,0,3,2:T(4,128)S(1)}, f32[4,32,10,1]{1,0,3,2:T(4,128)S(1)}, u32[]{:S(2)}, u32[]{:S(2)}) collective-permute-start(f32[4,32,10,1]{1,0,3,2:T(4,128)S(1)} %copy.75), channel_id=1, source_target_pairs={{1,0},{2,1},{3,2},{4,3},{5,4},{6,5},{7,6},{9,8},{10,9},{11,10},{12... | collective-permute-start | bytes 15368 | tf_op jit(solution)/shard_map/ppermute | solution.py:28
  86.4 5.5 %collective-permute-start.7 = (f32[4,32,10,1]{1,0,3,2:T(4,128)S(1)}, f32[4,32,10,1]{1,0,3,2:T(4,128)S(1)}, u32[]{:S(2)}, u32[]{:S(2)}) collective-permute-start(f32[4,32,10,1]{1,0,3,2:T(4,128)S(1)} %copy.77), channel_id=1, source_target_pairs={{0,1},{1,2},{2,3},{3,4},{4,5},{5,6},{6,7},{8,9},{9,10},{10,11},{11... | collective-permute-start | bytes 15368 | tf_op jit(solution)/shard_map/ppermute | solution.py:27
  93.9 2.1 %subtract_add_fusion.2 = f32[4,32,8,128]{3,2,1,0:T(8,128)S(1)} fusion(f32[4,31,8,128]{3,2,1,0:T(8,128)} %fusion.66, f32[4,32,10,1]{3,2,1,0:T(8,128)S(1)} %copy.76, f32[4,32,1,128]{3,2,1,0:T(1,128)S(1)} %collective-permute-done.4, f32[2,32,8,128]{3,2,1,0:T(8,128)S(1)} %slice.448, f32[1,32,8,128]{3,2,1,0:T(8,128)S(1)} %bitcast.219, ...), kind=kLoop, calls=%fused_computation.156 | loop fusion | flops 4456448 | bytes 1959936 | tf_op jit(solution)/shard_map/add | solution.py:54
  97.1 1.9 %collective-permute-start.8 = (f32[4,32,1,128]{3,2,1,0:T(1,128)S(1)}, f32[4,32,1,128]{3,2,1,0:T(1,128)S(1)}, u32[]{:S(2)}, u32[]{:S(2)}) collective-permute-start(f32[4,32,1,128]{3,2,1,0:T(1,128)S(1)} %get-tuple-element.36), channel_id=1, source_target_pairs={{8,0},{16,8},{24,16},{0,24},{9,1},{17,9},{25,17},{1,25},{10,2},{18... | collective-permute-start | bytes 196616 | tf_op jit(solution)/shard_map/ppermute | solution.py:28
  99.0 2.6 %collective-permute-start.9 = (f32[4,32,1,128]{3,2,1,0:T(1,128)S(1)}, f32[4,32,1,128]{3,2,1,0:T(1,128)S(1)}, u32[]{:S(2)}, u32[]{:S(2)}) collective-permute-start(f32[4,32,1,128]{3,2,1,0:T(1,128)S(1)} %get-tuple-element.35), channel_id=1, source_target_pairs={{0,8},{8,16},{16,24},{24,0},{1,9},{9,17},{17,25},{25,1},{2,10},{10... | collective-permute-start | bytes 196616 | tf_op jit(solution)/shard_map/ppermute | solution.py:27
  101.6 4.5 %collective-permute-done.9 = f32[4,32,1,128]{3,2,1,0:T(1,128)S(1)} collective-permute-done((f32[4,32,1,128]{3,2,1,0:T(1,128)S(1)}, f32[4,32,1,128]{3,2,1,0:T(1,128)S(1)}, u32[]{:S(2)}, u32[]{:S(2)}) %collective-permute-start.9) | collective-permute-done | bytes 65568 | tf_op jit(solution)/shard_map/ppermute | solution.py:27
  107.6 1.6 %copy.81 = f32[4,32,10,1]{1,0,3,2:T(4,128)S(1)} copy(f32[4,32,10,1]{3,2,1,0:T(8,128)} %get-tuple-element.28) | data formatting | bytes 10240 | tf_op jit(solution)/shard_map/slice | solution.py:26
  109.2 1.9 %collective-permute-start.10 = (f32[4,32,10,1]{1,0,3,2:T(4,128)S(1)}, f32[4,32,10,1]{1,0,3,2:T(4,128)S(1)}, u32[]{:S(2)}, u32[]{:S(2)}) collective-permute-start(f32[4,32,10,1]{1,0,3,2:T(4,128)S(1)} %copy.81), channel_id=1, source_target_pairs={{1,0},{2,1},{3,2},{4,3},{5,4},{6,5},{7,6},{9,8},{10,9},{11,10},{12... | collective-permute-start | bytes 15368 | tf_op jit(solution)/shard_map/ppermute | solution.py:28
  111.5 5.4 %collective-permute-start.11 = (f32[4,32,10,1]{1,0,3,2:T(4,128)S(1)}, f32[4,32,10,1]{1,0,3,2:T(4,128)S(1)}, u32[]{:S(2)}, u32[]{:S(2)}) collective-permute-start(f32[4,32,10,1]{1,0,3,2:T(4,128)S(1)} %copy.83), channel_id=1, source_target_pairs={{0,1},{1,2},{2,3},{3,4},{4,5},{5,6},{6,7},{8,9},{9,10},{10,11},{11... | collective-permute-start | bytes 15368 | tf_op jit(solution)/shard_map/ppermute | solution.py:27
  118.9 2.1 %subtract_add_fusion.1 = f32[4,32,8,128]{3,2,1,0:T(8,128)S(1)} fusion(f32[4,31,8,128]{3,2,1,0:T(8,128)} %fusion.65, f32[4,32,10,1]{3,2,1,0:T(8,128)S(1)} %copy.82, f32[4,32,1,128]{3,2,1,0:T(1,128)S(1)} %collective-permute-done.8, f32[2,32,8,128]{3,2,1,0:T(8,128)S(1)} %slice.461, f32[1,32,8,128]{3,2,1,0:T(8,128)S(1)} %bitcast.227, ...), kind=kLoop, calls=%fused_computation.155 | loop fusion | flops 4456448 | bytes 1959936 | tf_op jit(solution)/shard_map/add | solution.py:54
  122.8 1.9 %collective-permute-start.12 = (f32[4,32,1,128]{3,2,1,0:T(1,128)S(1)}, f32[4,32,1,128]{3,2,1,0:T(1,128)S(1)}, u32[]{:S(2)}, u32[]{:S(2)}) collective-permute-start(f32[4,32,1,128]{3,2,1,0:T(1,128)S(1)} %get-tuple-element.34), channel_id=1, source_target_pairs={{8,0},{16,8},{24,16},{0,24},{9,1},{17,9},{25,17},{1,25},{10,2},{18... | collective-permute-start | bytes 196616 | tf_op jit(solution)/shard_map/ppermute | solution.py:28
  124.7 2.4 %collective-permute-start.13 = (f32[4,32,1,128]{3,2,1,0:T(1,128)S(1)}, f32[4,32,1,128]{3,2,1,0:T(1,128)S(1)}, u32[]{:S(2)}, u32[]{:S(2)}) collective-permute-start(f32[4,32,1,128]{3,2,1,0:T(1,128)S(1)} %get-tuple-element.33), channel_id=1, source_target_pairs={{0,8},{8,16},{16,24},{24,0},{1,9},{9,17},{17,25},{25,1},{2,10},{10... | collective-permute-start | bytes 196616 | tf_op jit(solution)/shard_map/ppermute | solution.py:27
  127.2 4.7 %collective-permute-done.13 = f32[4,32,1,128]{3,2,1,0:T(1,128)S(1)} collective-permute-done((f32[4,32,1,128]{3,2,1,0:T(1,128)S(1)}, f32[4,32,1,128]{3,2,1,0:T(1,128)S(1)}, u32[]{:S(2)}, u32[]{:S(2)}) %collective-permute-start.13) | collective-permute-done | bytes 65568 | tf_op jit(solution)/shard_map/ppermute | solution.py:27
  133.4 1.9 %collective-permute-start.14 = (f32[4,32,10,1]{1,0,3,2:T(4,128)}, f32[4,32,10,1]{1,0,3,2:T(4,128)S(1)}, u32[]{:S(2)}, u32[]{:S(2)}) collective-permute-start(f32[4,32,10,1]{1,0,3,2:T(4,128)} %copy.87), channel_id=1, source_target_pairs={{1,0},{2,1},{3,2},{4,3},{5,4},{6,5},{7,6},{9,8},{10,9},{11,10},{12... | collective-permute-start | bytes 15368 | tf_op jit(solution)/shard_map/ppermute | solution.py:28
  135.7 5.4 %collective-permute-start.15 = (f32[4,32,10,1]{1,0,3,2:T(4,128)S(1)}, f32[4,32,10,1]{1,0,3,2:T(4,128)}, u32[]{:S(2)}, u32[]{:S(2)}) collective-permute-start(f32[4,32,10,1]{1,0,3,2:T(4,128)S(1)} %copy.89), channel_id=1, source_target_pairs={{0,1},{1,2},{2,3},{3,4},{4,5},{5,6},{6,7},{8,9},{9,10},{10,11},{11... | collective-permute-start | bytes 15368 | tf_op jit(solution)/shard_map/ppermute | solution.py:27
  143.8 1.8 %subtract_add_fusion = f32[4,32,8,128]{3,2,1,0:T(8,128)S(1)} fusion(f32[4,31,8,128]{3,2,1,0:T(8,128)S(1)} %fusion.64, f32[4,32,10,1]{3,2,1,0:T(8,128)S(1)} %copy.88, f32[4,32,1,128]{3,2,1,0:T(1,128)S(1)} %collective-permute-done.12, f32[2,32,8,128]{3,2,1,0:T(8,128)S(1)} %slice.474, f32[1,32,8,128]{3,2,1,0:T(8,128)S(1)} %bitcast.211, ...), kind=kLoop, calls=%fused_computation.154 | loop fusion | flops 4456448 | bytes 1959936 | tf_op jit(solution)/shard_map/add | solution.py:54
  (119 shorter events, 26.4 us)
Async XLA Ops:
  0.0 8.6 %copy-start.1 = (s32[16,1,16]{2,1,0:T(1,128)S(1)}, s32[16,1,16]{2,1,0:T(1,128)}, u32[]{:S(2)}) copy-start(s32[16,1,16]{2,1,0:T(1,128)} %param.5) | copy-start | bytes 3076
  0.0 23.6 %all-to-all-start = ((f32[16,8,8,128]{3,2,1,0:T(8,128)}), f32[16,8,8,128]{3,2,1,0:T(8,128)S(1)}, u32[]{:S(2)}, u32[]{:S(2)}) async-start(f32[16,8,8,128]{3,2,1,0:T(8,128)} %bitcast.229), calls=%async_computation | async-start | bytes 1048576 | tf_op jit(solution)/shard_map/all_to_all | solution.py:72
  25.5 20.0 %all-to-all-start.1 = ((f32[16,8,8,128]{3,2,1,0:T(8,128)}), f32[16,8,8,128]{3,2,1,0:T(8,128)S(1)}, u32[]{:S(2)}, u32[]{:S(2)}) async-start(f32[16,8,8,128]{3,2,1,0:T(8,128)} %select_select_fusion), calls=%async_computation.1 | async-start | bytes 1048576 | tf_op jit(solution)/shard_map/all_to_all | solution.py:78
  30.8 0.7 copy-start.2
  45.5 0.7 copy-start
  47.1 5.1 %collective-permute-start = (f32[4,32,1,128]{3,2,1,0:T(1,128)S(1)}, f32[4,32,1,128]{3,2,1,0:T(1,128)S(1)}, u32[]{:S(2)}, u32[]{:S(2)}) collective-permute-start(f32[4,32,1,128]{3,2,1,0:T(1,128)S(1)} %get-tuple-element.42), channel_id=1, source_target_pairs={{8,0},{16,8},{24,16},{0,24},{9,1},{17,9},{25,17},{1,25},{10,2},{18... | collective-permute-start | bytes 196616 | tf_op jit(solution)/shard_map/ppermute | solution.py:28
  50.2 7.1 %collective-permute-start.1 = (f32[4,32,1,128]{3,2,1,0:T(1,128)S(1)}, f32[4,32,1,128]{3,2,1,0:T(1,128)S(1)}, u32[]{:S(2)}, u32[]{:S(2)}) collective-permute-start(f32[4,32,1,128]{3,2,1,0:T(1,128)S(1)} %get-tuple-element.41), channel_id=1, source_target_pairs={{0,8},{8,16},{16,24},{24,0},{1,9},{9,17},{17,25},{25,1},{2,10},{10... | collective-permute-start | bytes 196616 | tf_op jit(solution)/shard_map/ppermute | solution.py:27
  58.3 7.8 %collective-permute-start.2 = (f32[4,32,10,1]{1,0,3,2:T(4,128)S(1)}, f32[4,32,10,1]{1,0,3,2:T(4,128)S(1)}, u32[]{:S(2)}, u32[]{:S(2)}) collective-permute-start(f32[4,32,10,1]{1,0,3,2:T(4,128)S(1)} %copy.69), channel_id=1, source_target_pairs={{1,0},{2,1},{3,2},{4,3},{5,4},{6,5},{7,6},{9,8},{10,9},{11,10},{12... | collective-permute-start | bytes 15368 | tf_op jit(solution)/shard_map/ppermute | solution.py:28
  60.6 6.9 %collective-permute-start.3 = (f32[4,32,10,1]{1,0,3,2:T(4,128)S(1)}, f32[4,32,10,1]{1,0,3,2:T(4,128)}, u32[]{:S(2)}, u32[]{:S(2)}) collective-permute-start(f32[4,32,10,1]{1,0,3,2:T(4,128)S(1)} %copy.71), channel_id=1, source_target_pairs={{0,1},{1,2},{2,3},{3,4},{4,5},{5,6},{6,7},{8,9},{9,10},{10,11},{11... | collective-permute-start | bytes 15368 | tf_op jit(solution)/shard_map/ppermute | solution.py:27
  72.0 4.3 %collective-permute-start.4 = (f32[4,32,1,128]{3,2,1,0:T(1,128)S(1)}, f32[4,32,1,128]{3,2,1,0:T(1,128)S(1)}, u32[]{:S(2)}, u32[]{:S(2)}) collective-permute-start(f32[4,32,1,128]{3,2,1,0:T(1,128)S(1)} %get-tuple-element.38), channel_id=1, source_target_pairs={{8,0},{16,8},{24,16},{0,24},{9,1},{17,9},{25,17},{1,25},{10,2},{18... | collective-permute-start | bytes 196616 | tf_op jit(solution)/shard_map/ppermute | solution.py:28
  73.9 7.1 %collective-permute-start.5 = (f32[4,32,1,128]{3,2,1,0:T(1,128)S(1)}, f32[4,32,1,128]{3,2,1,0:T(1,128)S(1)}, u32[]{:S(2)}, u32[]{:S(2)}) collective-permute-start(f32[4,32,1,128]{3,2,1,0:T(1,128)S(1)} %get-tuple-element.37), channel_id=1, source_target_pairs={{0,8},{8,16},{16,24},{24,0},{1,9},{9,17},{17,25},{25,1},{2,10},{10... | collective-permute-start | bytes 196616 | tf_op jit(solution)/shard_map/ppermute | solution.py:27
  84.1 8.7 %collective-permute-start.6 = (f32[4,32,10,1]{1,0,3,2:T(4,128)S(1)}, f32[4,32,10,1]{1,0,3,2:T(4,128)S(1)}, u32[]{:S(2)}, u32[]{:S(2)}) collective-permute-start(f32[4,32,10,1]{1,0,3,2:T(4,128)S(1)} %copy.75), channel_id=1, source_target_pairs={{1,0},{2,1},{3,2},{4,3},{5,4},{6,5},{7,6},{9,8},{10,9},{11,10},{12... | collective-permute-start | bytes 15368 | tf_op jit(solution)/shard_map/ppermute | solution.py:28
  86.4 7.0 %collective-permute-start.7 = (f32[4,32,10,1]{1,0,3,2:T(4,128)S(1)}, f32[4,32,10,1]{1,0,3,2:T(4,128)S(1)}, u32[]{:S(2)}, u32[]{:S(2)}) collective-permute-start(f32[4,32,10,1]{1,0,3,2:T(4,128)S(1)} %copy.77), channel_id=1, source_target_pairs={{0,1},{1,2},{2,3},{3,4},{4,5},{5,6},{6,7},{8,9},{9,10},{10,11},{11... | collective-permute-start | bytes 15368 | tf_op jit(solution)/shard_map/ppermute | solution.py:27
  97.1 4.5 %collective-permute-start.8 = (f32[4,32,1,128]{3,2,1,0:T(1,128)S(1)}, f32[4,32,1,128]{3,2,1,0:T(1,128)S(1)}, u32[]{:S(2)}, u32[]{:S(2)}) collective-permute-start(f32[4,32,1,128]{3,2,1,0:T(1,128)S(1)} %get-tuple-element.36), channel_id=1, source_target_pairs={{8,0},{16,8},{24,16},{0,24},{9,1},{17,9},{25,17},{1,25},{10,2},{18... | collective-permute-start | bytes 196616 | tf_op jit(solution)/shard_map/ppermute | solution.py:28
  99.0 7.1 %collective-permute-start.9 = (f32[4,32,1,128]{3,2,1,0:T(1,128)S(1)}, f32[4,32,1,128]{3,2,1,0:T(1,128)S(1)}, u32[]{:S(2)}, u32[]{:S(2)}) collective-permute-start(f32[4,32,1,128]{3,2,1,0:T(1,128)S(1)} %get-tuple-element.35), channel_id=1, source_target_pairs={{0,8},{8,16},{16,24},{24,0},{1,9},{9,17},{17,25},{25,1},{2,10},{10... | collective-permute-start | bytes 196616 | tf_op jit(solution)/shard_map/ppermute | solution.py:27
  109.2 8.6 %collective-permute-start.10 = (f32[4,32,10,1]{1,0,3,2:T(4,128)S(1)}, f32[4,32,10,1]{1,0,3,2:T(4,128)S(1)}, u32[]{:S(2)}, u32[]{:S(2)}) collective-permute-start(f32[4,32,10,1]{1,0,3,2:T(4,128)S(1)} %copy.81), channel_id=1, source_target_pairs={{1,0},{2,1},{3,2},{4,3},{5,4},{6,5},{7,6},{9,8},{10,9},{11,10},{12... | collective-permute-start | bytes 15368 | tf_op jit(solution)/shard_map/ppermute | solution.py:28
  111.5 6.9 %collective-permute-start.11 = (f32[4,32,10,1]{1,0,3,2:T(4,128)S(1)}, f32[4,32,10,1]{1,0,3,2:T(4,128)S(1)}, u32[]{:S(2)}, u32[]{:S(2)}) collective-permute-start(f32[4,32,10,1]{1,0,3,2:T(4,128)S(1)} %copy.83), channel_id=1, source_target_pairs={{0,1},{1,2},{2,3},{3,4},{4,5},{5,6},{6,7},{8,9},{9,10},{10,11},{11... | collective-permute-start | bytes 15368 | tf_op jit(solution)/shard_map/ppermute | solution.py:27
  122.8 4.3 %collective-permute-start.12 = (f32[4,32,1,128]{3,2,1,0:T(1,128)S(1)}, f32[4,32,1,128]{3,2,1,0:T(1,128)S(1)}, u32[]{:S(2)}, u32[]{:S(2)}) collective-permute-start(f32[4,32,1,128]{3,2,1,0:T(1,128)S(1)} %get-tuple-element.34), channel_id=1, source_target_pairs={{8,0},{16,8},{24,16},{0,24},{9,1},{17,9},{25,17},{1,25},{10,2},{18... | collective-permute-start | bytes 196616 | tf_op jit(solution)/shard_map/ppermute | solution.py:28
  124.7 7.1 %collective-permute-start.13 = (f32[4,32,1,128]{3,2,1,0:T(1,128)S(1)}, f32[4,32,1,128]{3,2,1,0:T(1,128)S(1)}, u32[]{:S(2)}, u32[]{:S(2)}) collective-permute-start(f32[4,32,1,128]{3,2,1,0:T(1,128)S(1)} %get-tuple-element.33), channel_id=1, source_target_pairs={{0,8},{8,16},{16,24},{24,0},{1,9},{9,17},{17,25},{25,1},{2,10},{10... | collective-permute-start | bytes 196616 | tf_op jit(solution)/shard_map/ppermute | solution.py:27
  133.4 7.9 %collective-permute-start.14 = (f32[4,32,10,1]{1,0,3,2:T(4,128)}, f32[4,32,10,1]{1,0,3,2:T(4,128)S(1)}, u32[]{:S(2)}, u32[]{:S(2)}) collective-permute-start(f32[4,32,10,1]{1,0,3,2:T(4,128)} %copy.87), channel_id=1, source_target_pairs={{1,0},{2,1},{3,2},{4,3},{5,4},{6,5},{7,6},{9,8},{10,9},{11,10},{12... | collective-permute-start | bytes 15368 | tf_op jit(solution)/shard_map/ppermute | solution.py:28
  135.7 6.9 %collective-permute-start.15 = (f32[4,32,10,1]{1,0,3,2:T(4,128)S(1)}, f32[4,32,10,1]{1,0,3,2:T(4,128)}, u32[]{:S(2)}, u32[]{:S(2)}) collective-permute-start(f32[4,32,10,1]{1,0,3,2:T(4,128)S(1)} %copy.89), channel_id=1, source_target_pairs={{0,1},{1,2},{2,3},{3,4},{4,5},{5,6},{6,7},{8,9},{9,10},{10,11},{11... | collective-permute-start | bytes 15368 | tf_op jit(solution)/shard_map/ppermute | solution.py:27

commit v2 on v1

--- a/solution.py
+++ b/solution.py
@@ -17,17 +17,24 @@
 CORIO_SLOPE = 0.1
 
 
-def extended(x, sides, width, wrap):
-    for axis, dim in sides:
-        size, length = (lax.axis_size(axis), x.shape[dim])
-        up = [(i, (i + 1) % size) for i in range(size if wrap else size - 1)]
-        down = [(j, i) for i, j in up]
-        last = lax.slice_in_dim(x, length - width, length, axis=dim)
-        leading = lax.slice_in_dim(x, 0, width, axis=dim)
-        before = lax.ppermute(last, axis, up)
-        after = lax.ppermute(leading, axis, down)
-        x = jnp.concatenate([before, x, after], axis=dim)
-    return x
+def shift_pairs(axis, wrap):
+    size = lax.axis_size(axis)
+    up = [(i, (i + 1) % size) for i in range(size if wrap else size - 1)]
+    return up, [(j, i) for i, j in up]
+
+
+def with_halo(x):
+    x_up, x_down = shift_pairs("gx", True)
+    y_up, y_down = shift_pairs("gy", False)
+    west = lax.ppermute(x[:, :, -1:, :], "gx", x_up)
+    east = lax.ppermute(x[:, :, :1, :], "gx", x_down)
+    south = lax.ppermute(x[:, :, :, -1:], "gy", y_up)
+    north = lax.ppermute(x[:, :, :, :1], "gy", y_down)
+    wide = jnp.concatenate([west, x, east], axis=2)
+    corner = ((0, 0), (0, 0), (1, 1), (0, 0))
+    return jnp.concatenate(
+        [jnp.pad(south, corner), wide, jnp.pad(north, corner)], axis=3
+    )
 
 
 def advance(padded, topmost_slab, eddy_diffusivity, coriolis):
@@ -89,8 +96,7 @@
     coriolis = coriolis_at(positions, total_rows)
     marine_variables = selected_particles
     for iteration in range(STEPS):
-        widened = extended(marine_variables, (("gx", 2),), 1, True)
-        padded = extended(widened, (("gy", 3),), 1, False)
+        padded = with_halo(marine_variables)
         marine_variables = advance(padded, topmost_slab, eddy_diffusivity, coriolis)
     return marine_variables[None]
 

time: 149 us -> 161 us (1.081)
  the two profiles are of different devices: /device:TPU:200 before, /device:TPU:14 now
where the time goes in v2:
time: 161 us; the launch traced here: 160 us
  waiting for transfers between devices  78.8 us (49%)
  starting transfers between devices  64.4 us (40%)
  other arithmetic  10.8 us (7%)
  local copies, waits for them, and re-layouts  5.79 us (4%)
    ppermute x4, waiting for transfers between devices, with_halo(): south = lax.ppermute(x[:, :, :, -1:], 'gy', y_up)  34.2 us
    ppermute x4, starting transfers between devices, with_halo(): east = lax.ppermute(x[:, :, :1, :], 'gx', x_down)  20.6 us
    ppermute x4, waiting for transfers between devices, with_halo(): north = lax.ppermute(x[:, :, :, :1], 'gy', y_down)  18.6 us
    ppermute x4, starting transfers between devices, with_halo(): south = lax.ppermute(x[:, :, :, -1:], 'gy', y_up)  17.3 us
    all_to_all x1, waiting for transfers between devices, resample(): back = lax.all_to_all(picked, 'dom', 0, 0, tiled=True)  14.2 us
    all_to_all x1, waiting for transfers between devices, resample(): by_member = lax.all_to_all(parts, 'dom', 0, 0, tiled=True)  11.8 us
    all_to_all x1, starting transfers between devices, resample(): by_member = lax.all_to_all(parts, 'dom', 0, 0, tiled=True)  8.6 us
    ppermute x4, starting transfers between devices, with_halo(): west = lax.ppermute(x[:, :, -1:, :], 'gx', x_up)  7.68 us
  transfers between devices with their start and end apart: 18, of which 10 were waited for; matrix products, arithmetic and copies ran while one was open for 3% of the time, Pallas kernels for 0%

profile of v2, /device:TPU:14, one launch (start us, length us, event | category | flops | bytes accessed | tf_op | source)
XLA Modules:
  0.0 160.4 jit_solution(1127755164951116061)
XLA Ops:
  0.0 8.6 %all-to-all-start = ((f32[16,8,8,128]{3,2,1,0:T(8,128)}), f32[16,8,8,128]{3,2,1,0:T(8,128)S(1)}, u32[]{:S(2)}, u32[]{:S(2)}) async-start(f32[16,8,8,128]{3,2,1,0:T(8,128)} %bitcast.223), calls=%async_computation | async-start | bytes 1048576 | tf_op jit(solution)/shard_map/all_to_all | solution.py:79
  11.9 11.8 %all-to-all-done = f32[16,8,8,128]{3,2,1,0:T(8,128)S(1)} async-done(((f32[16,8,8,128]{3,2,1,0:T(8,128)}), f32[16,8,8,128]{3,2,1,0:T(8,128)S(1)}, u32[]{:S(2)}, u32[]{:S(2)}) %all-to-all-start) | async-done | bytes 524320 | tf_op jit(solution)/shard_map/all_to_all | solution.py:79
  23.8 1.9 %select_select_fusion = f32[16,8,8,128]{3,2,1,0:T(8,128)} fusion(f32[8,8,128]{2,1,0:T(8,128)S(1)} %get-tuple-element.44, f32[8,8,128]{2,1,0:T(8,128)S(1)} %get-tuple-element.45, f32[8,8,128]{2,1,0:T(8,128)S(1)} %get-tuple-element.46, f32[8,8,128]{2,1,0:T(8,128)S(1)} %get-tuple-element.47, f32[8,8,128]{2,1,0:T(8,128)S(1)} %get-tuple-element.48, ...), kind=kLoop, calls=%fused_computation.154 | loop fusion | flops 2097152 | bytes 1081344 | tf_op jit(solution)/shard_map/jit(_where)/select_n | solution.py:84
  25.7 5.1 %all-to-all-start.1 = ((f32[16,8,8,128]{3,2,1,0:T(8,128)}), f32[16,8,8,128]{3,2,1,0:T(8,128)S(1)}, u32[]{:S(2)}, u32[]{:S(2)}) async-start(f32[16,8,8,128]{3,2,1,0:T(8,128)} %select_select_fusion), calls=%async_computation.1 | async-start | bytes 1048576 | tf_op jit(solution)/shard_map/all_to_all | solution.py:85
  31.6 14.2 %all-to-all-done.1 = f32[16,8,8,128]{3,2,1,0:T(8,128)S(1)} async-done(((f32[16,8,8,128]{3,2,1,0:T(8,128)}), f32[16,8,8,128]{3,2,1,0:T(8,128)S(1)}, u32[]{:S(2)}, u32[]{:S(2)}) %all-to-all-start.1) | async-done | bytes 524320 | tf_op jit(solution)/shard_map/all_to_all | solution.py:85
  46.1 1.9 %collective-permute-start.1 = (f32[4,32,1,128]{3,2,1,0:T(1,128)S(1)}, f32[4,32,1,128]{3,2,1,0:T(1,128)S(1)}, u32[]{:S(2)}, u32[]{:S(2)}) collective-permute-start(f32[4,32,1,128]{3,2,1,0:T(1,128)S(1)} %get-tuple-element.41), channel_id=1, source_target_pairs={{0,8},{8,16},{16,24},{24,0},{1,9},{9,17},{17,25},{25,1},{2,10},{10... | collective-permute-start | bytes 196616 | tf_op jit(solution)/shard_map/ppermute | solution.py:29
  48.0 5.1 %collective-permute-start = (f32[4,32,1,128]{3,2,1,0:T(1,128)S(1)}, f32[4,32,1,128]{3,2,1,0:T(1,128)S(1)}, u32[]{:S(2)}, u32[]{:S(2)}) collective-permute-start(f32[4,32,1,128]{3,2,1,0:T(1,128)S(1)} %get-tuple-element.42), channel_id=1, source_target_pairs={{8,0},{16,8},{24,16},{0,24},{9,1},{17,9},{25,17},{1,25},{10,2},{18... | collective-permute-start | bytes 196616 | tf_op jit(solution)/shard_map/ppermute | solution.py:30
  53.3 4.3 %collective-permute-start.3 = (f32[4,32,8,1]{3,2,1,0:T(8,128)S(1)}, f32[4,32,8,1]{3,2,1,0:T(8,128)S(1)}, u32[]{:S(2)}, u32[]{:S(2)}) collective-permute-start(f32[4,32,8,1]{3,2,1,0:T(8,128)S(1)} %get-tuple-element.39), channel_id=1, source_target_pairs={{0,1},{1,2},{2,3},{3,4},{4,5},{5,6},{6,7},{8,9},{9,10},{10,11},{11... | collective-permute-start | bytes 12296 | tf_op jit(solution)/shard_map/ppermute | solution.py:31
  57.6 1.3 collective-permute-start.2
  58.9 8.2 %collective-permute-done.3 = f32[4,32,8,1]{3,2,1,0:T(8,128)S(1)} collective-permute-done((f32[4,32,8,1]{3,2,1,0:T(8,128)S(1)}, f32[4,32,8,1]{3,2,1,0:T(8,128)S(1)}, u32[]{:S(2)}, u32[]{:S(2)}) %collective-permute-start.3) | collective-permute-done | bytes 4128 | tf_op jit(solution)/shard_map/ppermute | solution.py:31
  67.3 4.6 %collective-permute-done.2 = f32[4,32,8,1]{3,2,1,0:T(8,128)S(1)} collective-permute-done((f32[4,32,8,1]{3,2,1,0:T(8,128)S(1)}, f32[4,32,8,1]{3,2,1,0:T(8,128)S(1)}, u32[]{:S(2)}, u32[]{:S(2)}) %collective-permute-start.2) | collective-permute-done | bytes 4128 | tf_op jit(solution)/shard_map/ppermute | solution.py:32
  72.0 0.9 subtract_add_fusion.3
  74.3 1.9 %collective-permute-start.5 = (f32[4,32,1,128]{3,2,1,0:T(1,128)S(1)}, f32[4,32,1,128]{3,2,1,0:T(1,128)S(1)}, u32[]{:S(2)}, u32[]{:S(2)}) collective-permute-start(f32[4,32,1,128]{3,2,1,0:T(1,128)S(1)} %get-tuple-element.35), channel_id=1, source_target_pairs={{0,8},{8,16},{16,24},{24,0},{1,9},{9,17},{17,25},{25,1},{2,10},{10... | collective-permute-start | bytes 196616 | tf_op jit(solution)/shard_map/ppermute | solution.py:29
  76.2 5.1 %collective-permute-start.4 = (f32[4,32,1,128]{3,2,1,0:T(1,128)S(1)}, f32[4,32,1,128]{3,2,1,0:T(1,128)S(1)}, u32[]{:S(2)}, u32[]{:S(2)}) collective-permute-start(f32[4,32,1,128]{3,2,1,0:T(1,128)S(1)} %get-tuple-element.36), channel_id=1, source_target_pairs={{8,0},{16,8},{24,16},{0,24},{9,1},{17,9},{25,17},{1,25},{10,2},{18... | collective-permute-start | bytes 196616 | tf_op jit(solution)/shard_map/ppermute | solution.py:30
  81.3 4.3 %collective-permute-start.7 = (f32[4,32,8,1]{3,2,1,0:T(8,128)S(1)}, f32[4,32,8,1]{3,2,1,0:T(8,128)S(1)}, u32[]{:S(2)}, u32[]{:S(2)}) collective-permute-start(f32[4,32,8,1]{3,2,1,0:T(8,128)S(1)} %get-tuple-element.33), channel_id=1, source_target_pairs={{0,1},{1,2},{2,3},{3,4},{4,5},{5,6},{6,7},{8,9},{9,10},{10,11},{11... | collective-permute-start | bytes 12296 | tf_op jit(solution)/shard_map/ppermute | solution.py:31
  85.7 1.3 collective-permute-start.6
  87.1 8.9 %collective-permute-done.7 = f32[4,32,8,1]{3,2,1,0:T(8,128)S(1)} collective-permute-done((f32[4,32,8,1]{3,2,1,0:T(8,128)S(1)}, f32[4,32,8,1]{3,2,1,0:T(8,128)S(1)}, u32[]{:S(2)}, u32[]{:S(2)}) %collective-permute-start.7) | collective-permute-done | bytes 4128 | tf_op jit(solution)/shard_map/ppermute | solution.py:31
  96.1 5.9 %collective-permute-done.6 = f32[4,32,8,1]{3,2,1,0:T(8,128)S(1)} collective-permute-done((f32[4,32,8,1]{3,2,1,0:T(8,128)S(1)}, f32[4,32,8,1]{3,2,1,0:T(8,128)S(1)}, u32[]{:S(2)}, u32[]{:S(2)}) %collective-permute-start.6) | collective-permute-done | bytes 4128 | tf_op jit(solution)/shard_map/ppermute | solution.py:32
  102.1 0.9 subtract_add_fusion.2
  104.2 1.9 %collective-permute-start.9 = (f32[4,32,1,128]{3,2,1,0:T(1,128)S(1)}, f32[4,32,1,128]{3,2,1,0:T(1,128)S(1)}, u32[]{:S(2)}, u32[]{:S(2)}) collective-permute-start(f32[4,32,1,128]{3,2,1,0:T(1,128)S(1)} %get-tuple-element.31), channel_id=1, source_target_pairs={{0,8},{8,16},{16,24},{24,0},{1,9},{9,17},{17,25},{25,1},{2,10},{10... | collective-permute-start | bytes 196616 | tf_op jit(solution)/shard_map/ppermute | solution.py:29
  106.2 5.1 %collective-permute-start.8 = (f32[4,32,1,128]{3,2,1,0:T(1,128)S(1)}, f32[4,32,1,128]{3,2,1,0:T(1,128)S(1)}, u32[]{:S(2)}, u32[]{:S(2)}) collective-permute-start(f32[4,32,1,128]{3,2,1,0:T(1,128)S(1)} %get-tuple-element.32), channel_id=1, source_target_pairs={{8,0},{16,8},{24,16},{0,24},{9,1},{17,9},{25,17},{1,25},{10,2},{18... | collective-permute-start | bytes 196616 | tf_op jit(solution)/shard_map/ppermute | solution.py:30
  111.3 4.9 %collective-permute-start.11 = (f32[4,32,8,1]{3,2,1,0:T(8,128)S(1)}, f32[4,32,8,1]{3,2,1,0:T(8,128)S(1)}, u32[]{:S(2)}, u32[]{:S(2)}) collective-permute-start(f32[4,32,8,1]{3,2,1,0:T(8,128)S(1)} %get-tuple-element.29), channel_id=1, source_target_pairs={{0,1},{1,2},{2,3},{3,4},{4,5},{5,6},{6,7},{8,9},{9,10},{10,11},{11... | collective-permute-start | bytes 12296 | tf_op jit(solution)/shard_map/ppermute | solution.py:31
  116.2 1.3 collective-permute-start.10
  117.6 8.2 %collective-permute-done.11 = f32[4,32,8,1]{3,2,1,0:T(8,128)S(1)} collective-permute-done((f32[4,32,8,1]{3,2,1,0:T(8,128)S(1)}, f32[4,32,8,1]{3,2,1,0:T(8,128)S(1)}, u32[]{:S(2)}, u32[]{:S(2)}) %collective-permute-start.11) | collective-permute-done | bytes 4128 | tf_op jit(solution)/shard_map/ppermute | solution.py:31
  125.9 4.0 %collective-permute-done.10 = f32[4,32,8,1]{3,2,1,0:T(8,128)S(1)} collective-permute-done((f32[4,32,8,1]{3,2,1,0:T(8,128)S(1)}, f32[4,32,8,1]{3,2,1,0:T(8,128)S(1)}, u32[]{:S(2)}, u32[]{:S(2)}) %collective-permute-start.10) | collective-permute-done | bytes 4128 | tf_op jit(solution)/shard_map/ppermute | solution.py:32
  130.1 0.9 subtract_add_fusion.1
  132.3 1.9 %collective-permute-start.13 = (f32[4,32,1,128]{3,2,1,0:T(1,128)S(1)}, f32[4,32,1,128]{3,2,1,0:T(1,128)S(1)}, u32[]{:S(2)}, u32[]{:S(2)}) collective-permute-start(f32[4,32,1,128]{3,2,1,0:T(1,128)S(1)} %get-tuple-element.27), channel_id=1, source_target_pairs={{0,8},{8,16},{16,24},{24,0},{1,9},{9,17},{17,25},{25,1},{2,10},{10... | collective-permute-start | bytes 196616 | tf_op jit(solution)/shard_map/ppermute | solution.py:29
  134.2 5.1 %collective-permute-start.12 = (f32[4,32,1,128]{3,2,1,0:T(1,128)S(1)}, f32[4,32,1,128]{3,2,1,0:T(1,128)S(1)}, u32[]{:S(2)}, u32[]{:S(2)}) collective-permute-start(f32[4,32,1,128]{3,2,1,0:T(1,128)S(1)} %get-tuple-element.28), channel_id=1, source_target_pairs={{8,0},{16,8},{24,16},{0,24},{9,1},{17,9},{25,17},{1,25},{10,2},{18... | collective-permute-start | bytes 196616 | tf_op jit(solution)/shard_map/ppermute | solution.py:30
  139.3 3.8 %collective-permute-start.15 = (f32[4,32,8,1]{3,2,1,0:T(8,128)S(1)}, f32[4,32,8,1]{3,2,1,0:T(8,128)S(1)}, u32[]{:S(2)}, u32[]{:S(2)}) collective-permute-start(f32[4,32,8,1]{3,2,1,0:T(8,128)S(1)} %get-tuple-element.25), channel_id=1, source_target_pairs={{0,1},{1,2},{2,3},{3,4},{4,5},{5,6},{6,7},{8,9},{9,10},{10,11},{11... | collective-permute-start | bytes 12296 | tf_op jit(solution)/shard_map/ppermute | solution.py:31
  143.2 1.3 collective-permute-start.14
  144.6 8.9 %collective-permute-done.15 = f32[4,32,8,1]{3,2,1,0:T(8,128)S(1)} collective-permute-done((f32[4,32,8,1]{3,2,1,0:T(8,128)S(1)}, f32[4,32,8,1]{3,2,1,0:T(8,128)S(1)}, u32[]{:S(2)}, u32[]{:S(2)}) %collective-permute-start.15) | collective-permute-done | bytes 4128 | tf_op jit(solution)/shard_map/ppermute | solution.py:31
  153.6 4.0 %collective-permute-done.14 = f32[4,32,8,1]{3,2,1,0:T(8,128)S(1)} collective-permute-done((f32[4,32,8,1]{3,2,1,0:T(8,128)S(1)}, f32[4,32,8,1]{3,2,1,0:T(8,128)S(1)}, u32[]{:S(2)}, u32[]{:S(2)}) %collective-permute-start.14) | collective-permute-done | bytes 4128 | tf_op jit(solution)/shard_map/ppermute | solution.py:32
  (107 shorter events, 12.1 us)
Async XLA Ops:
  0.0 8.6 %copy-start.1 = (s32[16,1,16]{2,1,0:T(1,128)S(1)}, s32[16,1,16]{2,1,0:T(1,128)}, u32[]{:S(2)}) copy-start(s32[16,1,16]{2,1,0:T(1,128)} %param.5) | copy-start | bytes 3076
  0.0 23.8 %all-to-all-start = ((f32[16,8,8,128]{3,2,1,0:T(8,128)}), f32[16,8,8,128]{3,2,1,0:T(8,128)S(1)}, u32[]{:S(2)}, u32[]{:S(2)}) async-start(f32[16,8,8,128]{3,2,1,0:T(8,128)} %bitcast.223), calls=%async_computation | async-start | bytes 1048576 | tf_op jit(solution)/shard_map/all_to_all | solution.py:79
  25.7 20.1 %all-to-all-start.1 = ((f32[16,8,8,128]{3,2,1,0:T(8,128)}), f32[16,8,8,128]{3,2,1,0:T(8,128)S(1)}, u32[]{:S(2)}, u32[]{:S(2)}) async-start(f32[16,8,8,128]{3,2,1,0:T(8,128)} %select_select_fusion), calls=%async_computation.1 | async-start | bytes 1048576 | tf_op jit(solution)/shard_map/all_to_all | solution.py:85
  30.8 0.7 copy-start.2
  46.0 7.1 %copy-start = (f32[31]{0:T(128)S(1)}, f32[31]{0:T(128)}, u32[]{:S(2)}) copy-start(f32[31]{0:T(128)} %param.7) | copy-start | bytes 376
  46.1 26.0 %collective-permute-start.1 = (f32[4,32,1,128]{3,2,1,0:T(1,128)S(1)}, f32[4,32,1,128]{3,2,1,0:T(1,128)S(1)}, u32[]{:S(2)}, u32[]{:S(2)}) collective-permute-start(f32[4,32,1,128]{3,2,1,0:T(1,128)S(1)} %get-tuple-element.41), channel_id=1, source_target_pairs={{0,8},{8,16},{16,24},{24,0},{1,9},{9,17},{17,25},{25,1},{2,10},{10... | collective-permute-start | bytes 196616 | tf_op jit(solution)/shard_map/ppermute | solution.py:29
  48.0 24.1 %collective-permute-start = (f32[4,32,1,128]{3,2,1,0:T(1,128)S(1)}, f32[4,32,1,128]{3,2,1,0:T(1,128)S(1)}, u32[]{:S(2)}, u32[]{:S(2)}) collective-permute-start(f32[4,32,1,128]{3,2,1,0:T(1,128)S(1)} %get-tuple-element.42), channel_id=1, source_target_pairs={{8,0},{16,8},{24,16},{0,24},{9,1},{17,9},{25,17},{1,25},{10,2},{18... | collective-permute-start | bytes 196616 | tf_op jit(solution)/shard_map/ppermute | solution.py:30
  53.3 13.9 %collective-permute-start.3 = (f32[4,32,8,1]{3,2,1,0:T(8,128)S(1)}, f32[4,32,8,1]{3,2,1,0:T(8,128)S(1)}, u32[]{:S(2)}, u32[]{:S(2)}) collective-permute-start(f32[4,32,8,1]{3,2,1,0:T(8,128)S(1)} %get-tuple-element.39), channel_id=1, source_target_pairs={{0,1},{1,2},{2,3},{3,4},{4,5},{5,6},{6,7},{8,9},{9,10},{10,11},{11... | collective-permute-start | bytes 12296 | tf_op jit(solution)/shard_map/ppermute | solution.py:31
  57.6 14.3 %collective-permute-start.2 = (f32[4,32,8,1]{3,2,1,0:T(8,128)S(1)}, f32[4,32,8,1]{3,2,1,0:T(8,128)S(1)}, u32[]{:S(2)}, u32[]{:S(2)}) collective-permute-start(f32[4,32,8,1]{3,2,1,0:T(8,128)S(1)} %get-tuple-element.40), channel_id=1, source_target_pairs={{1,0},{2,1},{3,2},{4,3},{5,4},{6,5},{7,6},{9,8},{10,9},{11,10},{12... | collective-permute-start | bytes 12296 | tf_op jit(solution)/shard_map/ppermute | solution.py:32
  74.3 27.8 %collective-permute-start.5 = (f32[4,32,1,128]{3,2,1,0:T(1,128)S(1)}, f32[4,32,1,128]{3,2,1,0:T(1,128)S(1)}, u32[]{:S(2)}, u32[]{:S(2)}) collective-permute-start(f32[4,32,1,128]{3,2,1,0:T(1,128)S(1)} %get-tuple-element.35), channel_id=1, source_target_pairs={{0,8},{8,16},{16,24},{24,0},{1,9},{9,17},{17,25},{25,1},{2,10},{10... | collective-permute-start | bytes 196616 | tf_op jit(solution)/shard_map/ppermute | solution.py:29
  76.2 25.9 %collective-permute-start.4 = (f32[4,32,1,128]{3,2,1,0:T(1,128)S(1)}, f32[4,32,1,128]{3,2,1,0:T(1,128)S(1)}, u32[]{:S(2)}, u32[]{:S(2)}) collective-permute-start(f32[4,32,1,128]{3,2,1,0:T(1,128)S(1)} %get-tuple-element.36), channel_id=1, source_target_pairs={{8,0},{16,8},{24,16},{0,24},{9,1},{17,9},{25,17},{1,25},{10,2},{18... | collective-permute-start | bytes 196616 | tf_op jit(solution)/shard_map/ppermute | solution.py:30
  81.3 14.6 %collective-permute-start.7 = (f32[4,32,8,1]{3,2,1,0:T(8,128)S(1)}, f32[4,32,8,1]{3,2,1,0:T(8,128)S(1)}, u32[]{:S(2)}, u32[]{:S(2)}) collective-permute-start(f32[4,32,8,1]{3,2,1,0:T(8,128)S(1)} %get-tuple-element.33), channel_id=1, source_target_pairs={{0,1},{1,2},{2,3},{3,4},{4,5},{5,6},{6,7},{8,9},{9,10},{10,11},{11... | collective-permute-start | bytes 12296 | tf_op jit(solution)/shard_map/ppermute | solution.py:31
  85.7 16.3 %collective-permute-start.6 = (f32[4,32,8,1]{3,2,1,0:T(8,128)S(1)}, f32[4,32,8,1]{3,2,1,0:T(8,128)S(1)}, u32[]{:S(2)}, u32[]{:S(2)}) collective-permute-start(f32[4,32,8,1]{3,2,1,0:T(8,128)S(1)} %get-tuple-element.34), channel_id=1, source_target_pairs={{1,0},{2,1},{3,2},{4,3},{5,4},{6,5},{7,6},{9,8},{10,9},{11,10},{12... | collective-permute-start | bytes 12296 | tf_op jit(solution)/shard_map/ppermute | solution.py:32
  104.2 25.8 %collective-permute-start.9 = (f32[4,32,1,128]{3,2,1,0:T(1,128)S(1)}, f32[4,32,1,128]{3,2,1,0:T(1,128)S(1)}, u32[]{:S(2)}, u32[]{:S(2)}) collective-permute-start(f32[4,32,1,128]{3,2,1,0:T(1,128)S(1)} %get-tuple-element.31), channel_id=1, source_target_pairs={{0,8},{8,16},{16,24},{24,0},{1,9},{9,17},{17,25},{25,1},{2,10},{10... | collective-permute-start | bytes 196616 | tf_op jit(solution)/shard_map/ppermute | solution.py:29
  106.2 23.9 %collective-permute-start.8 = (f32[4,32,1,128]{3,2,1,0:T(1,128)S(1)}, f32[4,32,1,128]{3,2,1,0:T(1,128)S(1)}, u32[]{:S(2)}, u32[]{:S(2)}) collective-permute-start(f32[4,32,1,128]{3,2,1,0:T(1,128)S(1)} %get-tuple-element.32), channel_id=1, source_target_pairs={{8,0},{16,8},{24,16},{0,24},{9,1},{17,9},{25,17},{1,25},{10,2},{18... | collective-permute-start | bytes 196616 | tf_op jit(solution)/shard_map/ppermute | solution.py:30
  111.3 14.5 %collective-permute-start.11 = (f32[4,32,8,1]{3,2,1,0:T(8,128)S(1)}, f32[4,32,8,1]{3,2,1,0:T(8,128)S(1)}, u32[]{:S(2)}, u32[]{:S(2)}) collective-permute-start(f32[4,32,8,1]{3,2,1,0:T(8,128)S(1)} %get-tuple-element.29), channel_id=1, source_target_pairs={{0,1},{1,2},{2,3},{3,4},{4,5},{5,6},{6,7},{8,9},{9,10},{10,11},{11... | collective-permute-start | bytes 12296 | tf_op jit(solution)/shard_map/ppermute | solution.py:31
  116.2 13.7 %collective-permute-start.10 = (f32[4,32,8,1]{3,2,1,0:T(8,128)S(1)}, f32[4,32,8,1]{3,2,1,0:T(8,128)S(1)}, u32[]{:S(2)}, u32[]{:S(2)}) collective-permute-start(f32[4,32,8,1]{3,2,1,0:T(8,128)S(1)} %get-tuple-element.30), channel_id=1, source_target_pairs={{1,0},{2,1},{3,2},{4,3},{5,4},{6,5},{7,6},{9,8},{10,9},{11,10},{12... | collective-permute-start | bytes 12296 | tf_op jit(solution)/shard_map/ppermute | solution.py:32
  132.3 25.5 %collective-permute-start.13 = (f32[4,32,1,128]{3,2,1,0:T(1,128)S(1)}, f32[4,32,1,128]{3,2,1,0:T(1,128)S(1)}, u32[]{:S(2)}, u32[]{:S(2)}) collective-permute-start(f32[4,32,1,128]{3,2,1,0:T(1,128)S(1)} %get-tuple-element.27), channel_id=1, source_target_pairs={{0,8},{8,16},{16,24},{24,0},{1,9},{9,17},{17,25},{25,1},{2,10},{10... | collective-permute-start | bytes 196616 | tf_op jit(solution)/shard_map/ppermute | solution.py:29
  134.2 23.6 %collective-permute-start.12 = (f32[4,32,1,128]{3,2,1,0:T(1,128)S(1)}, f32[4,32,1,128]{3,2,1,0:T(1,128)S(1)}, u32[]{:S(2)}, u32[]{:S(2)}) collective-permute-start(f32[4,32,1,128]{3,2,1,0:T(1,128)S(1)} %get-tuple-element.28), channel_id=1, source_target_pairs={{8,0},{16,8},{24,16},{0,24},{9,1},{17,9},{25,17},{1,25},{10,2},{18... | collective-permute-start | bytes 196616 | tf_op jit(solution)/shard_map/ppermute | solution.py:30
  139.3 14.1 %collective-permute-start.15 = (f32[4,32,8,1]{3,2,1,0:T(8,128)S(1)}, f32[4,32,8,1]{3,2,1,0:T(8,128)S(1)}, u32[]{:S(2)}, u32[]{:S(2)}) collective-permute-start(f32[4,32,8,1]{3,2,1,0:T(8,128)S(1)} %get-tuple-element.25), channel_id=1, source_target_pairs={{0,1},{1,2},{2,3},{3,4},{4,5},{5,6},{6,7},{8,9},{9,10},{10,11},{11... | collective-permute-start | bytes 12296 | tf_op jit(solution)/shard_map/ppermute | solution.py:31
  143.2 14.4 %collective-permute-start.14 = (f32[4,32,8,1]{3,2,1,0:T(8,128)S(1)}, f32[4,32,8,1]{3,2,1,0:T(8,128)S(1)}, u32[]{:S(2)}, u32[]{:S(2)}) collective-permute-start(f32[4,32,8,1]{3,2,1,0:T(8,128)S(1)} %get-tuple-element.26), channel_id=1, source_target_pairs={{1,0},{2,1},{3,2},{4,3},{5,4},{6,5},{7,6},{9,8},{10,9},{11,10},{12... | collective-permute-start | bytes 12296 | tf_op jit(solution)/shard_map/ppermute | solution.py:32

commit v3 on v2

v3 whole, which is shorter than its diff:
```python
import jax
import jax.numpy as jnp
from jax import lax
from jax.sharding import PartitionSpec as P
from jax.experimental import pallas as pl
from jax.experimental.pallas import tpu as pltpu

STEPS = 4
TILE = 8


ADVECT = 0.2
DIFFUSE = 0.15
BUOY_TEMP = 0.2
BUOY_SALT = 0.1
PRESS_SCALE = 0.25
WIND_SCALE = 0.2
CORIO_BASE = 0.1
CORIO_SLOPE = 0.1


HALO = STEPS


def shift_pairs(axis, wrap):
    size = lax.axis_size(axis)
    up = [(i, (i + 1) % size) for i in range(size if wrap else size - 1)]
    return up, [(j, i) for i, j in up]


def with_wide_halo(packed, lanes):
    x_up, x_down = shift_pairs("gx", True)
    width_x = packed.shape[1]
    west = lax.ppermute(packed[:, width_x - HALO:, :], "gx", x_up)
    east = lax.ppermute(packed[:, :HALO, :], "gx", x_down)
    rows = jnp.concatenate([packed, east, west], axis=1)
    y_up, y_down = shift_pairs("gy", False)
    width_y = rows.shape[2]
    south = lax.ppermute(rows[:, :, width_y - HALO:], "gy", y_up)
    north = lax.ppermute(rows[:, :, :HALO], "gy", y_down)
    gap = jnp.zeros(rows.shape[:2] + (lanes - width_y - 2 * HALO,), rows.dtype)
    return jnp.concatenate([rows, north, gap, south], axis=2)


def forecast_kernel(levels, eddy_ref, cor_ref, mask_ref, full_ref, out_ref, buf0, buf1):
    cor = cor_ref[...]
    inside = mask_ref[...] > 0.5
    rows, lanes = full_ref.shape[1], full_ref.shape[2]
    state_rows = 4 * levels
    drag0 = WIND_SCALE * full_ref[state_rows]
    drag1 = WIND_SCALE * full_ref[state_rows + 1]

    def around(a):
        return (
            pltpu.roll(a, rows - 1, 0),
            pltpu.roll(a, 1, 0),
            pltpu.roll(a, lanes - 1, 1),
            pltpu.roll(a, 1, 1),
        )

    def one_step(src, dst, last):
        def level(k, total):
            above = jnp.minimum(k + 1, levels - 1)
            below = jnp.maximum(k - 1, 0)
            c = [src[f * levels + k] for f in range(4)]
            up = [src[f * levels + above] for f in range(4)]
            dn = [src[f * levels + below] for f in range(4)]
            e_up = eddy_ref[k + 1]
            e_dn = eddy_ref[k]
            total = total + (BUOY_TEMP * c[2] - BUOY_SALT * c[3])
            pressure = PRESS_SCALE * total
            east_vel, north_vel = c[0], c[1]
            new = []
            for f in range(4):
                e, w, n, s = around(c[f])
                grad_x = 0.5 * (e - w)
                grad_y = 0.5 * (n - s)
                spread = e + w + n + s - 4.0 * c[f]
                vertical = e_up * (up[f] - c[f]) - e_dn * (c[f] - dn[f])
                carried = east_vel * grad_x + north_vel * grad_y
                new.append(c[f] - ADVECT * carried + DIFFUSE * spread + vertical)
            pe, pw, pn, ps = around(pressure)
            top = jnp.where(k == 0, 1.0, 0.0).astype(jnp.float32)
            new[0] = new[0] + cor * north_vel - 0.5 * (pe - pw) + drag0 * top
            new[1] = new[1] - cor * east_vel - 0.5 * (pn - ps) + drag1 * top
            for f in range(4):
                if last:
                    out_ref[f * levels + k] = new[f][: out_ref.shape[1], : out_ref.shape[2]]
                else:
                    dst[f * levels + k] = jnp.where(inside, new[f], 0.0)
            return total

        lax.fori_loop(0, levels, level, jnp.zeros((rows, lanes), jnp.float32))

    bufs = (buf0, buf1)
    src = full_ref
    for step in range(STEPS):
        dst = bufs[step % 2]
        one_step(src, dst, step == STEPS - 1)
        src = dst


def forecast(full, eddy, cor, inside, levels, width_x, width_y):
    state_rows, rows, lanes = 4 * levels, full.shape[1], full.shape[2]
    kernel = lambda *refs: forecast_kernel(levels, *refs)
    vmem = pl.BlockSpec(memory_space=pltpu.VMEM)
    cells = state_rows * rows * lanes
    return pl.pallas_call(
        kernel,
        out_shape=jax.ShapeDtypeStruct((state_rows, width_x, width_y), jnp.float32),
        in_specs=[pl.BlockSpec(memory_space=pltpu.SMEM), vmem, vmem, vmem],
        out_specs=vmem,
        scratch_shapes=[pltpu.VMEM((state_rows, rows, lanes), jnp.float32)] * 2,
        cost_estimate=pl.CostEstimate(
            flops=STEPS * cells * 40, transcendentals=0, bytes_accessed=full.size * 4 + state_rows * width_x * width_y * 4
        ),
    )(eddy, cor, inside, full)


def coriolis_at(positions, total_rows):
    return CORIO_BASE + CORIO_SLOPE * (positions.astype(jnp.float32) + 0.5) / total_rows


def resample(ensemble, ancestors):
    members = lax.axis_size("dom")
    block = ensemble[0]
    fields, levels, width_x, width_y = block.shape
    groups = fields * levels // members
    parts = block.reshape(members, groups, width_x, width_y)
    by_member = lax.all_to_all(parts, "dom", 0, 0, tiled=True)
    tiles = ancestors[:, 0, :]
    cell_source = jnp.repeat(tiles, TILE, 1)[:, None, None, :]
    picked = jnp.zeros_like(by_member)
    for member in range(members):
        picked = jnp.where(cell_source == member, by_member[member][None], picked)
    back = lax.all_to_all(picked, "dom", 0, 0, tiled=True)
    return back.reshape(fields, levels, width_x, width_y)


def per_device(ensemble, ancestors, particle_air_drag, eddy_diffusivity):
    _, fields, levels, width_x, width_y = ensemble.shape
    selected = resample(ensemble, ancestors)
    packed = jnp.concatenate(
        [selected.reshape(fields * levels, width_x, width_y), particle_air_drag[0]], axis=0
    )
    lanes = 2 * width_y
    full = with_wide_halo(packed, lanes)
    lane = jnp.arange(lanes, dtype=jnp.int32)
    offset = jnp.where(lane < width_y + 2 * HALO + (lanes - width_y - 2 * HALO) // 2, lane, lane - lanes)
    row_block = lax.axis_index("gy")
    total_rows = width_y * lax.axis_size("gy")
    positions = row_block * width_y + offset
    cor = coriolis_at(positions, total_rows)[None]
    used = (offset < width_y + HALO) & (offset >= -HALO)
    inside = (used & (positions >= 0) & (positions < total_rows)).astype(jnp.float32)[None]
    zero = jnp.zeros((1,), jnp.float32)
    eddy = jnp.concatenate([zero, eddy_diffusivity, zero])
    out = forecast(full, eddy, cor, inside, levels, width_x, width_y)
    return out.reshape(1, fields, levels, width_x, width_y)


def solution(mesh):
    placed = (
        P("dom", None, None, "gx", "gy"),
        P(None, "gx", "gy"),
        P("dom", None, "gx", "gy"),
        P(),
    )
    return jax.shard_map(
        per_device,
        mesh=mesh,
        in_specs=placed,
        out_specs=P("dom", None, None, "gx", "gy"),
        check_vma=False,
    )
```

time: 161 us -> 87.8 us (0.55)
  the two profiles are of different devices: /device:TPU:14 before, /device:TPU:200 now
where the time goes in v3:
time: 87.8 us; the launch traced here: 87.4 us
  starting transfers between devices  21 us (24%)
  blocking collectives  19.8 us (23%)
  waiting for transfers between devices  17.6 us (20%)
  Pallas kernels  16.8 us (19%)
  local copies, waits for them, and re-layouts  6.45 us (7%)
  other arithmetic  5.59 us (6%)
    all_to_all x1, blocking collectives, resample(): back = lax.all_to_all(picked, 'dom', 0, 0, tiled=True)  19.8 us
    pallas_call x1, Pallas kernels, forecast(): pl.pallas_call(kernel, out_shape=jax.ShapeDtypeStruct((state_rows, width_...  16.8 us
    all_to_all x1, waiting for transfers between devices, resample(): by_member = lax.all_to_all(parts, 'dom', 0, 0, tiled=True)  11 us
    all_to_all x1, starting transfers between devices, resample(): by_member = lax.all_to_all(parts, 'dom', 0, 0, tiled=True)  8.49 us
    ppermute x1, starting transfers between devices, with_wide_halo(): south = lax.ppermute(rows[:, :, width_y - HALO:], 'gy', y_up)  5.49 us
    ppermute x1, waiting for transfers between devices, with_wide_halo(): west = lax.ppermute(packed[:, width_x - HALO:, :], 'gx', x_up)  5.33 us
    ppermute x1, starting transfers between devices, with_wide_halo(): east = lax.ppermute(packed[:, :HALO, :], 'gx', x_down)  3.17 us
    eq x48, local copies, waits for them, and re-layouts, resample(): picked = jnp.where(cell_source == member, by_member[member][None], picked)  3.06 us
  transfers between devices with their start and end apart: 5, of which 4 were waited for; matrix products, arithmetic and copies ran while one was open for 8% of the time, Pallas kernels for 0%

profile of v3, /device:TPU:200, one launch (start us, length us, event | category | flops | bytes accessed | tf_op | source)
XLA Modules:
  0.0 87.4 jit_solution(16646155589388277164)
XLA Ops:
  0.0 8.5 %all-to-all-start = ((f32[16,8,8,128]{3,2,1,0:T(8,128)}), f32[16,8,8,128]{3,2,1,0:T(8,128)S(1)}, u32[]{:S(2)}, u32[]{:S(2)}) async-start(f32[16,8,8,128]{3,2,1,0:T(8,128)} %bitcast.87), calls=%async_computation | async-start | bytes 1048576 | tf_op jit(solution)/shard_map/all_to_all | solution.py:130
  8.5 0.8 broadcast_compare_fusion.15
  9.3 0.1 copy.73
  9.4 0.1 copy.74
  9.6 0.1 copy.75
  9.9 0.1 copy.78
  10.2 0.1 copy.81
  11.7 0.1 copy.85
  11.9 0.1 copy.86
  12.1 0.1 copy.87
  12.3 0.1 copy.88
  12.5 11.0 %all-to-all-done = f32[16,8,8,128]{3,2,1,0:T(8,128)S(1)} async-done(((f32[16,8,8,128]{3,2,1,0:T(8,128)}), f32[16,8,8,128]{3,2,1,0:T(8,128)S(1)}, u32[]{:S(2)}, u32[]{:S(2)}) %all-to-all-start) | async-done | bytes 524320 | tf_op jit(solution)/shard_map/all_to_all | solution.py:130
  23.5 1.1 %select_select_fusion = f32[16,8,8,128]{3,2,1,0:T(8,128)S(1)} fusion(f32[8,8,128]{2,1,0:T(8,128)S(1)} %get-tuple-element.10, f32[8,8,128]{2,1,0:T(8,128)S(1)} %get-tuple-element.11, f32[8,8,128]{2,1,0:T(8,128)S(1)} %get-tuple-element.12, f32[8,8,128]{2,1,0:T(8,128)S(1)} %get-tuple-element.13, f32[8,8,128]{2,1,0:T(8,128)S(1)} %get-tuple-element.14, ...), kind=kLoop, calls=%fused_computation.4 | loop fusion | flops 2097152 | bytes 1081344 | tf_op jit(solution)/shard_map/jit(_where)/select_n | solution.py:135
  24.6 19.8 %all_to_all.10 = f32[16,8,8,128]{3,2,1,0:T(8,128)S(1)} all-to-all(f32[16,8,8,128]{3,2,1,0:T(8,128)S(1)} %select_select_fusion), channel_id=1, replica_groups=mesh['dom'=16,'gx'=4,'gy'=8] {'dom'}, dimensions={0} | all-to-all | bytes 1048576 | tf_op jit(solution)/shard_map/all_to_all | solution.py:136
  44.5 3.2 %collective-permute-start = (f32[130,4,128]{2,1,0:T(4,128)S(1)}, f32[130,4,128]{2,1,0:T(4,128)S(1)}, u32[]{:S(2)}, u32[]{:S(2)}) collective-permute-start(f32[130,4,128]{2,1,0:T(4,128)S(1)} %get-tuple-element.7), channel_id=1, source_target_pairs={{8,0},{16,8},{24,16},{0,24},{9,1},{17,9},{25,17},{1,25},{10,2},{18... | collective-permute-start | bytes 798728 | tf_op jit(solution)/shard_map/ppermute | solution.py:35
  47.7 1.9 %collective-permute-start.1 = (f32[130,4,128]{2,1,0:T(4,128)S(1)}, f32[130,4,128]{2,1,0:T(4,128)S(1)}, u32[]{:S(2)}, u32[]{:S(2)}) collective-permute-start(f32[130,4,128]{2,1,0:T(4,128)S(1)} %get-tuple-element.8), channel_id=1, source_target_pairs={{0,8},{8,16},{16,24},{24,0},{1,9},{9,17},{17,25},{25,1},{2,10},{10... | collective-permute-start | bytes 798728 | tf_op jit(solution)/shard_map/ppermute | solution.py:34
  49.6 0.5 and_convert_fusion.refs_2_
  50.1 0.6 multiply_add_fusion.refs_1_
  50.7 0.9 %collective-permute-done = f32[130,4,128]{2,1,0:T(4,128)S(1)} collective-permute-done((f32[130,4,128]{2,1,0:T(4,128)S(1)}, f32[130,4,128]{2,1,0:T(4,128)S(1)}, u32[]{:S(2)}, u32[]{:S(2)}) %collective-permute-start) | collective-permute-done | bytes 266272 | tf_op jit(solution)/shard_map/ppermute | solution.py:35
  51.6 5.3 %collective-permute-done.1 = f32[130,4,128]{2,1,0:T(4,128)S(1)} collective-permute-done((f32[130,4,128]{2,1,0:T(4,128)S(1)}, f32[130,4,128]{2,1,0:T(4,128)S(1)}, u32[]{:S(2)}, u32[]{:S(2)}) %collective-permute-start.1) | collective-permute-done | bytes 266272 | tf_op jit(solution)/shard_map/ppermute | solution.py:34
  56.9 0.1 pad_maximum_fusion.1
  57.0 0.3 fusion.1
  57.4 0.7 copy.69
  58.1 1.9 %collective-permute-start.2 = (f32[130,16,4]{0,1,2:T(8,128)S(1)}, f32[130,16,4]{0,1,2:T(8,128)S(1)}, u32[]{:S(2)}, u32[]{:S(2)}) collective-permute-start(f32[130,16,4]{0,1,2:T(8,128)S(1)} %copy.69), channel_id=1, source_target_pairs={{1,0},{2,1},{3,2},{4,3},{5,4},{6,5},{7,6},{9,8},{10,9},{11,10},{12... | collective-permute-start | bytes 99848 | tf_op jit(solution)/shard_map/ppermute | solution.py:40
  60.0 0.7 copy.70
  60.7 5.5 %collective-permute-start.3 = (f32[130,16,4]{0,1,2:T(8,128)S(1)}, f32[130,16,4]{0,1,2:T(8,128)S(1)}, u32[]{:S(2)}, u32[]{:S(2)}) collective-permute-start(f32[130,16,4]{0,1,2:T(8,128)S(1)} %copy.70), channel_id=1, source_target_pairs={{0,1},{1,2},{2,3},{3,4},{4,5},{5,6},{6,7},{8,9},{9,10},{10,11},{11... | collective-permute-start | bytes 99848 | tf_op jit(solution)/shard_map/ppermute | solution.py:39
  66.2 0.6 pad_maximum_fusion.3.refs_0_
  66.9 0.8 copy.71
  67.6 0.4 collective-permute-done.3
  68.1 0.8 copy.72
  68.9 1.8 %pad_maximum_fusion.refs_3_ = f32[130,16,256]{2,1,0:T(8,128)} fusion(f32[130,16,4]{2,1,0:T(8,128)S(1)} %copy.72, f32[130,16,4]{2,1,0:T(8,128)S(1)} %copy.71, f32[130,4,128]{2,1,0:T(4,128)S(1)} %collective-permute-done.1, f32[130,4,128]{2,1,0:T(4,128)S(1)} %collective-permute-done, f32[2,8,128]{2,1,0:T(8,128)S(1)} %bitcast.90, f32[128,8,128]{2,1,0:T(8,128)S(1)} %bitcast.86, ...), kind=kLoop, calls=%fused_computation | loop fusion | flops 3194880 | bytes 3262464 | tf_op jit(solution)/shard_map/concatenate | solution.py:42
  70.6 16.8 %shard_map.46 = f32[128,8,128]{2,1,0:T(8,128)} custom-call(f32[33]{0:T(128)} %pad_maximum_fusion.3.refs_0_, f32[1,256]{1,0:T(1,128)} %multiply_add_fusion.refs_1_, f32[1,256]{1,0:T(1,128)} %and_convert_fusion.refs_2_, f32[130,16,256]{2,1,0:T(8,128)} %pad_maximum_fusion.refs_3_), custom_call_target="tpu_custom_call" | custom-call | flops 83886080 | bytes 2654208 | tf_op jit(solution)/shard_map/pallas_call | solution.py:108
  (48 shorter events, 2.4 us)
Async XLA Ops:
  0.0 23.5 %all-to-all-start = ((f32[16,8,8,128]{3,2,1,0:T(8,128)}), f32[16,8,8,128]{3,2,1,0:T(8,128)S(1)}, u32[]{:S(2)}, u32[]{:S(2)}) async-start(f32[16,8,8,128]{3,2,1,0:T(8,128)} %bitcast.87), calls=%async_computation | async-start | bytes 1048576 | tf_op jit(solution)/shard_map/all_to_all | solution.py:130
  23.5 20.9 %copy-start = (f32[1,2,8,128]{3,2,1,0:T(8,128)S(1)}, f32[1,2,8,128]{3,2,1,0:T(8,128)}, u32[]{:S(2)}) copy-start(f32[1,2,8,128]{3,2,1,0:T(8,128)} %param.6) | copy-start | bytes 24580
  44.5 7.1 %collective-permute-start = (f32[130,4,128]{2,1,0:T(4,128)S(1)}, f32[130,4,128]{2,1,0:T(4,128)S(1)}, u32[]{:S(2)}, u32[]{:S(2)}) collective-permute-start(f32[130,4,128]{2,1,0:T(4,128)S(1)} %get-tuple-element.7), channel_id=1, source_target_pairs={{8,0},{16,8},{24,16},{0,24},{9,1},{17,9},{25,17},{1,25},{10,2},{18... | collective-permute-start | bytes 798728 | tf_op jit(solution)/shard_map/ppermute | solution.py:35
  47.7 9.2 %collective-permute-start.1 = (f32[130,4,128]{2,1,0:T(4,128)S(1)}, f32[130,4,128]{2,1,0:T(4,128)S(1)}, u32[]{:S(2)}, u32[]{:S(2)}) collective-permute-start(f32[130,4,128]{2,1,0:T(4,128)S(1)} %get-tuple-element.8), channel_id=1, source_target_pairs={{0,8},{8,16},{16,24},{24,0},{1,9},{9,17},{17,25},{25,1},{2,10},{10... | collective-permute-start | bytes 798728 | tf_op jit(solution)/shard_map/ppermute | solution.py:34
  57.4 8.8 %copy-start.1 = (f32[31]{0:T(128)S(1)}, f32[31]{0:T(128)}, u32[]{:S(2)}) copy-start(f32[31]{0:T(128)} %param.7) | copy-start | bytes 376
  58.1 8.8 %collective-permute-start.2 = (f32[130,16,4]{0,1,2:T(8,128)S(1)}, f32[130,16,4]{0,1,2:T(8,128)S(1)}, u32[]{:S(2)}, u32[]{:S(2)}) collective-permute-start(f32[130,16,4]{0,1,2:T(8,128)S(1)} %copy.69), channel_id=1, source_target_pairs={{1,0},{2,1},{3,2},{4,3},{5,4},{6,5},{7,6},{9,8},{10,9},{11,10},{12... | collective-permute-start | bytes 99848 | tf_op jit(solution)/shard_map/ppermute | solution.py:40
  60.7 7.4 %collective-permute-start.3 = (f32[130,16,4]{0,1,2:T(8,128)S(1)}, f32[130,16,4]{0,1,2:T(8,128)S(1)}, u32[]{:S(2)}, u32[]{:S(2)}) collective-permute-start(f32[130,16,4]{0,1,2:T(8,128)S(1)} %copy.70), channel_id=1, source_target_pairs={{0,1},{1,2},{2,3},{3,4},{4,5},{5,6},{6,7},{8,9},{9,10},{10,11},{11... | collective-permute-start | bytes 99848 | tf_op jit(solution)/shard_map/ppermute | solution.py:39

commit v4 on v3

v4 whole, which is shorter than its diff:
```python
import jax
import jax.numpy as jnp
from jax import lax
from jax.sharding import PartitionSpec as P
from jax.experimental import pallas as pl
from jax.experimental.pallas import tpu as pltpu

STEPS = 4
TILE = 8


ADVECT = 0.2
DIFFUSE = 0.15
BUOY_TEMP = 0.2
BUOY_SALT = 0.1
PRESS_SCALE = 0.25
WIND_SCALE = 0.2
CORIO_BASE = 0.1
CORIO_SLOPE = 0.1


HALO = STEPS


def shift_pairs(axis, wrap):
    size = lax.axis_size(axis)
    up = [(i, (i + 1) % size) for i in range(size if wrap else size - 1)]
    return up, [(j, i) for i, j in up]


def halo_pieces(packed):
    x_up, x_down = shift_pairs("gx", True)
    width_x = packed.shape[1]
    west = lax.ppermute(packed[:, width_x - HALO:, :], "gx", x_up)
    east = lax.ppermute(packed[:, :HALO, :], "gx", x_down)
    rows = jnp.concatenate([packed, east, west], axis=1)
    y_up, y_down = shift_pairs("gy", False)
    width_y = rows.shape[2]
    south = lax.ppermute(rows[:, :, width_y - HALO:], "gy", y_up)
    north = lax.ppermute(rows[:, :, :HALO], "gy", y_down)
    return east, west, north, south


def forecast_kernel(levels, eddy_ref, cor_ref, mask_ref, centre_ref, east_ref,
                    west_ref, north_ref, south_ref, out_ref, buf0, buf1):
    n_rows, lanes = buf0.shape[1], buf0.shape[2]
    wx, wy = centre_ref.shape[1], centre_ref.shape[2]
    buf0[:, :wx, :wy] = centre_ref[...]
    buf0[:, wx:wx + HALO, :wy] = east_ref[...]
    buf0[:, wx + HALO:, :wy] = west_ref[...]
    buf0[:, :, wy:] = jnp.zeros((buf0.shape[0], n_rows, lanes - wy), jnp.float32)
    buf0[:, :, wy:wy + HALO] = north_ref[...]
    buf0[:, :, lanes - HALO:] = south_ref[...]

    cor = cor_ref[...]
    inside = mask_ref[...] > 0.5
    state_rows = 4 * levels
    drag = [WIND_SCALE * buf0[state_rows + i] for i in range(2)]

    def around(a):
        return (
            pltpu.roll(a, n_rows - 1, 0),
            pltpu.roll(a, 1, 0),
            pltpu.roll(a, lanes - 1, 1),
            pltpu.roll(a, 1, 1),
        )

    row8 = lax.broadcasted_iota(jnp.int32, (wx, wy), 0)
    lane8 = lax.broadcasted_iota(jnp.int32, (wx, wy), 1)

    def around_block(lo, nx, hi):
        return (
            jnp.where(row8 == wx - 1, pltpu.roll(nx, wx - 1, 0), pltpu.roll(lo, wx - 1, 0)),
            jnp.where(row8 == 0, pltpu.roll(nx, 1, 0), pltpu.roll(lo, 1, 0)),
            jnp.where(lane8 == wy - 1, pltpu.roll(hi, wy - 1, 1), pltpu.roll(lo, wy - 1, 1)),
            jnp.where(lane8 == 0, pltpu.roll(hi, 1, 1), pltpu.roll(lo, 1, 1)),
        )

    def tendencies(k, c, up, dn, nb, total, nbt, cor_k, drag_k):
        e_up = eddy_ref[k + 1]
        e_dn = eddy_ref[k]
        east_vel, north_vel = c[0], c[1]
        new = []
        for f in range(4):
            e, w, n, s = nb[f]
            spread = e + w + n + s - 4.0 * c[f]
            vertical = e_up * (up[f] - c[f]) - e_dn * (c[f] - dn[f])
            carried = east_vel * (e - w) + north_vel * (n - s)
            new.append(c[f] - (0.5 * ADVECT) * carried + DIFFUSE * spread + vertical)
        pe, pw, pn, ps = nbt
        top = jnp.where(k == 0, 1.0, 0.0).astype(jnp.float32)
        new[0] = new[0] + cor_k * north_vel - (0.5 * PRESS_SCALE) * (pe - pw) + drag_k[0] * top
        new[1] = new[1] - cor_k * east_vel - (0.5 * PRESS_SCALE) * (pn - ps) + drag_k[1] * top
        return new

    def one_step(src, dst):
        def level(k, total):
            above = jnp.minimum(k + 1, levels - 1)
            below = jnp.maximum(k - 1, 0)
            c = [src[f * levels + k] for f in range(4)]
            up = [src[f * levels + above] for f in range(4)]
            dn = [src[f * levels + below] for f in range(4)]
            total = total + (BUOY_TEMP * c[2] - BUOY_SALT * c[3])
            nb = [around(c[f]) for f in range(4)]
            new = tendencies(k, c, up, dn, nb, total, around(total), cor, drag)
            for f in range(4):
                dst[f * levels + k] = jnp.where(inside, new[f], 0.0)
            return total

        lax.fori_loop(0, levels, level, jnp.zeros((n_rows, lanes), jnp.float32))

    def last_step(src):
        def pieces(i):
            return (src[i, :wx, :wy], src[i, wx:, :wy], src[i, :wx, wy:])

        drag_b = [d[:wx, :wy] for d in drag]
        cor_b = cor[:, :wy]

        def level(k, totals):
            above = jnp.minimum(k + 1, levels - 1)
            below = jnp.maximum(k - 1, 0)
            cp = [pieces(f * levels + k) for f in range(4)]
            c = [p[0] for p in cp]
            up = [src[f * levels + above, :wx, :wy] for f in range(4)]
            dn = [src[f * levels + below, :wx, :wy] for f in range(4)]
            totals = tuple(
                t + (BUOY_TEMP * a - BUOY_SALT * b) for t, a, b in zip(totals, cp[2], cp[3])
            )
            nb = [around_block(*p) for p in cp]
            new = tendencies(k, c, up, dn, nb, totals[0], around_block(*totals), cor_b, drag_b)
            for f in range(4):
                out_ref[f * levels + k] = new[f]
            return totals

        zero = jnp.zeros((wx, wy), jnp.float32)
        lax.fori_loop(0, levels, level, (zero, zero, zero))

    one_step(buf0, buf1)
    one_step(buf1, buf0)
    one_step(buf0, buf1)
    last_step(buf1)


def forecast(pieces, eddy, cor, inside, levels):
    centre = pieces[0]
    packed_rows, width_x, width_y = centre.shape
    state_rows = 4 * levels
    rows, lanes = width_x + 2 * HALO, 2 * width_y
    kernel = lambda *refs: forecast_kernel(levels, *refs)
    vmem = pl.BlockSpec(memory_space=pltpu.VMEM)
    cells = state_rows * rows * lanes
    return pl.pallas_call(
        kernel,
        out_shape=jax.ShapeDtypeStruct((state_rows, width_x, width_y), jnp.float32),
        in_specs=[pl.BlockSpec(memory_space=pltpu.SMEM)] + [vmem] * 7,
        out_specs=vmem,
        scratch_shapes=[
            pltpu.VMEM((packed_rows, rows, lanes), jnp.float32),
            pltpu.VMEM((state_rows, rows, lanes), jnp.float32),
        ],
        cost_estimate=pl.CostEstimate(
            flops=STEPS * cells * 40, transcendentals=0,
            bytes_accessed=2 * centre.size * 4 + state_rows * width_x * width_y * 4,
        ),
    )(eddy, cor, inside, *pieces)


def coriolis_at(positions, total_rows):
    return CORIO_BASE + CORIO_SLOPE * (positions.astype(jnp.float32) + 0.5) / total_rows


def resample(ensemble, ancestors):
    members = lax.axis_size("dom")
    block = ensemble[0]
    fields, levels, width_x, width_y = block.shape
    groups = fields * levels // members
    parts = block.reshape(members, groups, width_x, width_y)
    by_member = lax.all_to_all(parts, "dom", 0, 0, tiled=True)
    tiles = ancestors[:, 0, :]
    cell_source = jnp.repeat(tiles, TILE, 1)[:, None, None, :]
    picked = jnp.zeros_like(by_member)
    for member in range(members):
        picked = jnp.where(cell_source == member, by_member[member][None], picked)
    back = lax.all_to_all(picked, "dom", 0, 0, tiled=True)
    return back.reshape(fields, levels, width_x, width_y)


def per_device(ensemble, ancestors, particle_air_drag, eddy_diffusivity):
    _, fields, levels, width_x, width_y = ensemble.shape
    selected = resample(ensemble, ancestors)
    packed = jnp.concatenate(
        [selected.reshape(fields * levels, width_x, width_y), particle_air_drag[0]], axis=0
    )
    lanes = 2 * width_y
    pieces = (packed,) + halo_pieces(packed)
    lane = jnp.arange(lanes, dtype=jnp.int32)
    offset = jnp.where(lane < width_y + 2 * HALO + (lanes - width_y - 2 * HALO) // 2, lane, lane - lanes)
    row_block = lax.axis_index("gy")
    total_rows = width_y * lax.axis_size("gy")
    positions = row_block * width_y + offset
    cor = coriolis_at(positions, total_rows)[None]
    used = (offset < width_y + HALO) & (offset >= -HALO)
    inside = (used & (positions >= 0) & (positions < total_rows)).astype(jnp.float32)[None]
    zero = jnp.zeros((1,), jnp.float32)
    eddy = jnp.concatenate([zero, eddy_diffusivity, zero])
    out = forecast(pieces, eddy, cor, inside, levels)
    return out.reshape(1, fields, levels, width_x, width_y)


def solution(mesh):
    placed = (
        P("dom", None, None, "gx", "gy"),
        P(None, "gx", "gy"),
        P("dom", None, "gx", "gy"),
        P(),
    )
    return jax.shard_map(
        per_device,
        mesh=mesh,
        in_specs=placed,
        out_specs=P("dom", None, None, "gx", "gy"),
        check_vma=False,
    )
```

time: 87.8 us -> 89 us (1.014)
  local copies, waits for them, and re-layouts: 6.45 us -> 8.76 us
  waiting for transfers between devices: 17.6 us -> 16.4 us
  Pallas kernels: 16.8 us -> 17.7 us
    ppermute x2, local copies, waits for them, and re-layouts: 1.57 us -> 3.4 us  [the longest x1 1.7 us: halo_pieces(): south = lax.ppermute(rows[:, :, width_y - HALO:], 'gy', y_up)]
    concatenate x2 -> x1, other arithmetic: 1.92 us -> 0.13 us  [halo_pieces(): rows = jnp.concatenate([packed, east, west], axis=1)]
    ppermute x4, waiting for transfers between devices: 6.62 us -> 5.45 us  [the longest x1 5.32 us: halo_pieces(): west = lax.ppermute(packed[:, width_x - HALO:, :], 'gx', x_up)]
  transfers between devices with their start and end apart: 5 -> 5, of which waited for: 4 -> 3; matrix products, arithmetic and copies ran while one was open for 8% -> 10% of each run, Pallas kernels for 0% -> 0%
where the time goes in v4:
time: 89 us; the launch traced here: 88.7 us
  starting transfers between devices  21 us (24%)
  blocking collectives  19.8 us (22%)
  Pallas kernels  17.7 us (20%)
  waiting for transfers between devices  16.4 us (18%)
  local copies, waits for them, and re-layouts  8.76 us (10%)
  other arithmetic  4.83 us (5%)
    all_to_all x1, blocking collectives, resample(): back = lax.all_to_all(picked, 'dom', 0, 0, tiled=True)  19.8 us
    pallas_call x1, Pallas kernels, forecast(): pl.pallas_call(kernel, out_shape=jax.ShapeDtypeStruct((state_rows, width_...  17.7 us
    all_to_all x1, waiting for transfers between devices, resample(): by_member = lax.all_to_all(parts, 'dom', 0, 0, tiled=True)  11 us
    all_to_all x1, starting transfers between devices, resample(): by_member = lax.all_to_all(parts, 'dom', 0, 0, tiled=True)  8.49 us
    ppermute x1, starting transfers between devices, halo_pieces(): south = lax.ppermute(rows[:, :, width_y - HALO:], 'gy', y_up)  5.49 us
    ppermute x1, waiting for transfers between devices, halo_pieces(): west = lax.ppermute(packed[:, width_x - HALO:, :], 'gx', x_up)  5.32 us
    ppermute x1, starting transfers between devices, halo_pieces(): east = lax.ppermute(packed[:, :HALO, :], 'gx', x_down)  3.17 us
    eq x48, local copies, waits for them, and re-layouts, resample(): picked = jnp.where(cell_source == member, by_member[member][None], picked)  3.06 us
  transfers between devices with their start and end apart: 5, of which 3 were waited for; matrix products, arithmetic and copies ran while one was open for 10% of the time, Pallas kernels for 0%

profile of v4, /device:TPU:200, one launch (start us, length us, event | category | flops | bytes accessed | tf_op | source)
XLA Modules:
  0.0 88.7 jit_solution(5992703147569556476)
XLA Ops:
  0.0 8.5 %all-to-all-start = ((f32[16,8,8,128]{3,2,1,0:T(8,128)}), f32[16,8,8,128]{3,2,1,0:T(8,128)S(1)}, u32[]{:S(2)}, u32[]{:S(2)}) async-start(f32[16,8,8,128]{3,2,1,0:T(8,128)} %bitcast.87), calls=%async_computation | async-start | bytes 1048576 | tf_op jit(solution)/shard_map/all_to_all | solution.py:178
  8.5 0.8 broadcast_compare_fusion.15
  9.3 0.1 copy.73
  9.4 0.1 copy.74
  9.6 0.1 copy.75
  9.9 0.1 copy.78
  10.2 0.1 copy.81
  11.7 0.1 copy.85
  11.9 0.1 copy.86
  12.1 0.1 copy.87
  12.3 0.1 copy.88
  12.5 11.0 %all-to-all-done = f32[16,8,8,128]{3,2,1,0:T(8,128)S(1)} async-done(((f32[16,8,8,128]{3,2,1,0:T(8,128)}), f32[16,8,8,128]{3,2,1,0:T(8,128)S(1)}, u32[]{:S(2)}, u32[]{:S(2)}) %all-to-all-start) | async-done | bytes 524320 | tf_op jit(solution)/shard_map/all_to_all | solution.py:178
  23.5 1.1 %select_select_fusion = f32[16,8,8,128]{3,2,1,0:T(8,128)S(1)} fusion(f32[8,8,128]{2,1,0:T(8,128)S(1)} %get-tuple-element.10, f32[8,8,128]{2,1,0:T(8,128)S(1)} %get-tuple-element.11, f32[8,8,128]{2,1,0:T(8,128)S(1)} %get-tuple-element.12, f32[8,8,128]{2,1,0:T(8,128)S(1)} %get-tuple-element.13, f32[8,8,128]{2,1,0:T(8,128)S(1)} %get-tuple-element.14, ...), kind=kLoop, calls=%fused_computation.4 | loop fusion | flops 2097152 | bytes 1081344 | tf_op jit(solution)/shard_map/jit(_where)/select_n | solution.py:183
  24.6 19.8 %all_to_all.10 = f32[16,8,8,128]{3,2,1,0:T(8,128)S(1)} all-to-all(f32[16,8,8,128]{3,2,1,0:T(8,128)S(1)} %select_select_fusion), channel_id=1, replica_groups=mesh['dom'=16,'gx'=4,'gy'=8] {'dom'}, dimensions={0} | all-to-all | bytes 1048576 | tf_op jit(solution)/shard_map/all_to_all | solution.py:184
  44.5 3.2 %collective-permute-start = (f32[130,4,128]{2,1,0:T(4,128)S(1)}, f32[130,4,128]{2,1,0:T(4,128)S(1)}, u32[]{:S(2)}, u32[]{:S(2)}) collective-permute-start(f32[130,4,128]{2,1,0:T(4,128)S(1)} %get-tuple-element.8), channel_id=1, source_target_pairs={{8,0},{16,8},{24,16},{0,24},{9,1},{17,9},{25,17},{1,25},{10,2},{18... | collective-permute-start | bytes 798728 | tf_op jit(solution)/shard_map/ppermute | solution.py:35
  47.7 1.9 %collective-permute-start.1 = (f32[130,4,128]{2,1,0:T(4,128)S(1)}, f32[130,4,128]{2,1,0:T(4,128)S(1)}, u32[]{:S(2)}, u32[]{:S(2)}) collective-permute-start(f32[130,4,128]{2,1,0:T(4,128)S(1)} %get-tuple-element.7), channel_id=1, source_target_pairs={{0,8},{8,16},{16,24},{24,0},{1,9},{9,17},{17,25},{25,1},{2,10},{10... | collective-permute-start | bytes 798728 | tf_op jit(solution)/shard_map/ppermute | solution.py:34
  49.6 0.7 pad_maximum_fusion.2.refs_0_
  50.3 0.6 and_convert_fusion.refs_2_
  50.9 0.6 multiply_add_fusion.refs_1_
  51.5 0.1 collective-permute-done.refs_4_
  51.6 5.3 %collective-permute-done.1.refs_5_ = f32[130,4,128]{2,1,0:T(4,128)S(1)} collective-permute-done((f32[130,4,128]{2,1,0:T(4,128)S(1)}, f32[130,4,128]{2,1,0:T(4,128)S(1)}, u32[]{:S(2)}, u32[]{:S(2)}) %collective-permute-start.1) | collective-permute-done | bytes 266272 | tf_op jit(solution)/shard_map/ppermute | solution.py:34
  56.9 0.1 pad_maximum_fusion
  57.1 0.6 copy-done.1
  57.6 0.3 fusion.2
  58.0 0.7 copy.69
  58.6 1.9 %collective-permute-start.2 = (f32[130,16,4]{0,1,2:T(8,128)S(1)}, f32[130,16,4]{0,1,2:T(8,128)S(1)}, u32[]{:S(2)}, u32[]{:S(2)}) collective-permute-start(f32[130,16,4]{0,1,2:T(8,128)S(1)} %copy.69), channel_id=1, source_target_pairs={{1,0},{2,1},{3,2},{4,3},{5,4},{6,5},{7,6},{9,8},{10,9},{11,10},{12... | collective-permute-start | bytes 99848 | tf_op jit(solution)/shard_map/ppermute | solution.py:40
  60.6 0.7 copy.70
  61.2 5.5 %collective-permute-start.3 = (f32[130,16,4]{0,1,2:T(8,128)S(1)}, f32[130,16,4]{0,1,2:T(8,128)S(1)}, u32[]{:S(2)}, u32[]{:S(2)}) collective-permute-start(f32[130,16,4]{0,1,2:T(8,128)S(1)} %copy.70), channel_id=1, source_target_pairs={{0,1},{1,2},{2,3},{3,4},{4,5},{5,6},{6,7},{8,9},{9,10},{10,11},{11... | collective-permute-start | bytes 99848 | tf_op jit(solution)/shard_map/ppermute | solution.py:39
  66.7 0.9 pad_maximum_fusion.1.refs_3_
  67.6 1.7 %copy.71.refs_6_ = f32[130,16,4]{2,1,0:T(8,128)} copy(f32[130,16,4]{0,1,2:T(8,128)S(1)} %collective-permute-done.2) | data formatting | bytes 66560 | tf_op jit(solution)/shard_map/ppermute | solution.py:40
  69.3 1.7 %copy.72.refs_7_ = f32[130,16,4]{2,1,0:T(8,128)} copy(f32[130,16,4]{0,1,2:T(8,128)S(1)} %collective-permute-done.3) | data formatting | bytes 66560 | tf_op jit(solution)/shard_map/ppermute | solution.py:39
  71.0 17.7 %shard_map.46 = f32[128,8,128]{2,1,0:T(8,128)} custom-call(f32[33]{0:T(128)} %pad_maximum_fusion.2.refs_0_, f32[1,256]{1,0:T(1,128)} %multiply_add_fusion.refs_1_, f32[1,256]{1,0:T(1,128)} %and_convert_fusion.refs_2_, f32[130,8,128]{2,1,0:T(8,128)} %pad_maximum_fusion.1.refs_3_, f32[130,4,128]{2,1,0:T(4,128)} %copy-done, f32[130,4,128]{2,1,0:T(4,128)} %copy-done.1, ...), custom_call_target="tpu_custom_call" | custom-call | flops 83886080 | bytes 1589248 | tf_op jit(solution)/shard_map/pallas_call | solution.py:152
  (50 shorter events, 2.3 us)
Async XLA Ops:
  0.0 23.5 %all-to-all-start = ((f32[16,8,8,128]{3,2,1,0:T(8,128)}), f32[16,8,8,128]{3,2,1,0:T(8,128)S(1)}, u32[]{:S(2)}, u32[]{:S(2)}) async-start(f32[16,8,8,128]{3,2,1,0:T(8,128)} %bitcast.87), calls=%async_computation | async-start | bytes 1048576 | tf_op jit(solution)/shard_map/all_to_all | solution.py:178
  23.5 20.9 %copy-start.2 = (f32[1,2,8,128]{3,2,1,0:T(8,128)S(1)}, f32[1,2,8,128]{3,2,1,0:T(8,128)}, u32[]{:S(2)}) copy-start(f32[1,2,8,128]{3,2,1,0:T(8,128)} %param.6) | copy-start | bytes 24580
  24.6 25.0 %copy-start.3 = (f32[31]{0:T(128)S(1)}, f32[31]{0:T(128)}, u32[]{:S(2)}) copy-start(f32[31]{0:T(128)} %param.7) | copy-start | bytes 376
  44.5 7.1 %collective-permute-start = (f32[130,4,128]{2,1,0:T(4,128)S(1)}, f32[130,4,128]{2,1,0:T(4,128)S(1)}, u32[]{:S(2)}, u32[]{:S(2)}) collective-permute-start(f32[130,4,128]{2,1,0:T(4,128)S(1)} %get-tuple-element.8), channel_id=1, source_target_pairs={{8,0},{16,8},{24,16},{0,24},{9,1},{17,9},{25,17},{1,25},{10,2},{18... | collective-permute-start | bytes 798728 | tf_op jit(solution)/shard_map/ppermute | solution.py:35
  47.7 9.2 %collective-permute-start.1 = (f32[130,4,128]{2,1,0:T(4,128)S(1)}, f32[130,4,128]{2,1,0:T(4,128)S(1)}, u32[]{:S(2)}, u32[]{:S(2)}) collective-permute-start(f32[130,4,128]{2,1,0:T(4,128)S(1)} %get-tuple-element.7), channel_id=1, source_target_pairs={{0,8},{8,16},{16,24},{24,0},{1,9},{9,17},{17,25},{25,1},{2,10},{10... | collective-permute-start | bytes 798728 | tf_op jit(solution)/shard_map/ppermute | solution.py:34
  51.6 5.5 %copy-start = (f32[130,4,128]{2,1,0:T(4,128)}, f32[130,4,128]{2,1,0:T(4,128)S(1)}, u32[]{:S(2)}) copy-start(f32[130,4,128]{2,1,0:T(4,128)S(1)} %collective-permute-done.refs_4_) | copy-start | bytes 798724
  56.9 0.7 copy-start.1
  58.6 9.0 %collective-permute-start.2 = (f32[130,16,4]{0,1,2:T(8,128)S(1)}, f32[130,16,4]{0,1,2:T(8,128)S(1)}, u32[]{:S(2)}, u32[]{:S(2)}) collective-permute-start(f32[130,16,4]{0,1,2:T(8,128)S(1)} %copy.69), channel_id=1, source_target_pairs={{1,0},{2,1},{3,2},{4,3},{5,4},{6,5},{7,6},{9,8},{10,9},{11,10},{12... | collective-permute-start | bytes 99848 | tf_op jit(solution)/shard_map/ppermute | solution.py:40
  61.2 8.1 %collective-permute-start.3 = (f32[130,16,4]{0,1,2:T(8,128)S(1)}, f32[130,16,4]{0,1,2:T(8,128)S(1)}, u32[]{:S(2)}, u32[]{:S(2)}) collective-permute-start(f32[130,16,4]{0,1,2:T(8,128)S(1)} %copy.70), channel_id=1, source_target_pairs={{0,1},{1,2},{2,3},{3,4},{4,5},{5,6},{6,7},{8,9},{9,10},{10,11},{11... | collective-permute-start | bytes 99848 | tf_op jit(solution)/shard_map/ppermute | solution.py:39

commit v5 on v4

--- a/solution.py
+++ b/solution.py
@@ -28,7 +28,7 @@
     return up, [(j, i) for i, j in up]
 
 
-def halo_pieces(packed):
+def with_wide_halo(packed, lanes):
     x_up, x_down = shift_pairs("gx", True)
     width_x = packed.shape[1]
     west = lax.ppermute(packed[:, width_x - HALO:, :], "gx", x_up)
@@ -38,24 +38,18 @@
     width_y = rows.shape[2]
     south = lax.ppermute(rows[:, :, width_y - HALO:], "gy", y_up)
     north = lax.ppermute(rows[:, :, :HALO], "gy", y_down)
-    return east, west, north, south
-
-
-def forecast_kernel(levels, eddy_ref, cor_ref, mask_ref, centre_ref, east_ref,
-                    west_ref, north_ref, south_ref, out_ref, buf0, buf1):
-    n_rows, lanes = buf0.shape[1], buf0.shape[2]
-    wx, wy = centre_ref.shape[1], centre_ref.shape[2]
-    buf0[:, :wx, :wy] = centre_ref[...]
-    buf0[:, wx:wx + HALO, :wy] = east_ref[...]
-    buf0[:, wx + HALO:, :wy] = west_ref[...]
-    buf0[:, :, wy:] = jnp.zeros((buf0.shape[0], n_rows, lanes - wy), jnp.float32)
-    buf0[:, :, wy:wy + HALO] = north_ref[...]
-    buf0[:, :, lanes - HALO:] = south_ref[...]
+    gap = jnp.zeros(rows.shape[:2] + (lanes - width_y - 2 * HALO,), rows.dtype)
+    return jnp.concatenate([rows, north, gap, south], axis=2)
+
+
+def forecast_kernel(levels, eddy_ref, cor_ref, mask_ref, full_ref, out_ref, buf0, buf1):
+    n_rows, lanes = full_ref.shape[1], full_ref.shape[2]
+    wx, wy = out_ref.shape[1], out_ref.shape[2]
 
     cor = cor_ref[...]
     inside = mask_ref[...] > 0.5
     state_rows = 4 * levels
-    drag = [WIND_SCALE * buf0[state_rows + i] for i in range(2)]
+    drag = [WIND_SCALE * full_ref[state_rows + i] for i in range(2)]
 
     def around(a):
         return (
@@ -135,34 +129,28 @@
         zero = jnp.zeros((wx, wy), jnp.float32)
         lax.fori_loop(0, levels, level, (zero, zero, zero))
 
-    one_step(buf0, buf1)
+    one_step(full_ref, buf1)
     one_step(buf1, buf0)
     one_step(buf0, buf1)
     last_step(buf1)
 
 
-def forecast(pieces, eddy, cor, inside, levels):
-    centre = pieces[0]
-    packed_rows, width_x, width_y = centre.shape
-    state_rows = 4 * levels
-    rows, lanes = width_x + 2 * HALO, 2 * width_y
+def forecast(full, eddy, cor, inside, levels, width_x, width_y):
+    state_rows, rows, lanes = 4 * levels, full.shape[1], full.shape[2]
     kernel = lambda *refs: forecast_kernel(levels, *refs)
     vmem = pl.BlockSpec(memory_space=pltpu.VMEM)
     cells = state_rows * rows * lanes
     return pl.pallas_call(
         kernel,
         out_shape=jax.ShapeDtypeStruct((state_rows, width_x, width_y), jnp.float32),
-        in_specs=[pl.BlockSpec(memory_space=pltpu.SMEM)] + [vmem] * 7,
+        in_specs=[pl.BlockSpec(memory_space=pltpu.SMEM), vmem, vmem, vmem],
         out_specs=vmem,
-        scratch_shapes=[
-            pltpu.VMEM((packed_rows, rows, lanes), jnp.float32),
-            pltpu.VMEM((state_rows, rows, lanes), jnp.float32),
-        ],
+        scratch_shapes=[pltpu.VMEM((state_rows, rows, lanes), jnp.float32)] * 2,
         cost_estimate=pl.CostEstimate(
             flops=STEPS * cells * 40, transcendentals=0,
-            bytes_accessed=2 * centre.size * 4 + state_rows * width_x * width_y * 4,
+            bytes_accessed=full.size * 4 + state_rows * width_x * width_y * 4,
         ),
-    )(eddy, cor, inside, *pieces)
+    )(eddy, cor, inside, full)
 
 
 def coriolis_at(positions, total_rows):
@@ -192,7 +180,7 @@
         [selected.reshape(fields * levels, width_x, width_y), particle_air_drag[0]], axis=0
     )
     lanes = 2 * width_y
-    pieces = (packed,) + halo_pieces(packed)
+    full = with_wide_halo(packed, lanes)
     lane = jnp.arange(lanes, dtype=jnp.int32)
     offset = jnp.where(lane < width_y + 2 * HALO + (lanes - width_y - 2 * HALO) // 2, lane, lane - lanes)
     row_block = lax.axis_index("gy")
@@ -203,7 +191,7 @@
     inside = (used & (positions >= 0) & (positions < total_rows)).astype(jnp.float32)[None]
     zero = jnp.zeros((1,), jnp.float32)
     eddy = jnp.concatenate([zero, eddy_diffusivity, zero])
-    out = forecast(pieces, eddy, cor, inside, levels)
+    out = forecast(full, eddy, cor, inside, levels, width_x, width_y)
     return out.reshape(1, fields, levels, width_x, width_y)
 
 

time: 89 us -> 87.9 us (0.988)
  local copies, waits for them, and re-layouts: 8.76 us -> 6.45 us
  waiting for transfers between devices: 16.4 us -> 17.6 us
    ppermute x2, local copies, waits for them, and re-layouts: 3.4 us -> 1.57 us  [the longest x1 0.78 us: with_wide_halo(): north = lax.ppermute(rows[:, :, :HALO], 'gy', y_down)]
    concatenate x1 -> x2, other arithmetic: 0.13 us -> 1.92 us  [the longest x1 1.79 us: with_wide_halo(): return jnp.concatenate([rows, north, gap, south], axis=2)]
    ppermute x4, waiting for transfers between devices: 5.45 us -> 6.62 us  [the longest x1 5.33 us: with_wide_halo(): west = lax.ppermute(packed[:, width_x - HALO:, :], 'gx', x_up)]
  transfers between devices with their start and end apart: 5 -> 5, of which waited for: 3 -> 4; matrix products, arithmetic and copies ran while one was open for 10% -> 8% of each run, Pallas kernels for 0% -> 0%
where the time goes in v5:
time: 87.9 us; the launch traced here: 87.5 us
  starting transfers between devices  21 us (24%)
  blocking collectives  19.8 us (23%)
  waiting for transfers between devices  17.6 us (20%)
  Pallas kernels  16.9 us (19%)
  local copies, waits for them, and re-layouts  6.45 us (7%)
  other arithmetic  5.59 us (6%)
    all_to_all x1, blocking collectives, resample(): back = lax.all_to_all(picked, 'dom', 0, 0, tiled=True)  19.8 us
    pallas_call x1, Pallas kernels, forecast(): pl.pallas_call(kernel, out_shape=jax.ShapeDtypeStruct((state_rows, width_...  16.9 us
    all_to_all x1, waiting for transfers between devices, resample(): by_member = lax.all_to_all(parts, 'dom', 0, 0, tiled=True)  11 us
    all_to_all x1, starting transfers between devices, resample(): by_member = lax.all_to_all(parts, 'dom', 0, 0, tiled=True)  8.49 us
    ppermute x1, starting transfers between devices, with_wide_halo(): south = lax.ppermute(rows[:, :, width_y - HALO:], 'gy', y_up)  5.49 us
    ppermute x1, waiting for transfers between devices, with_wide_halo(): west = lax.ppermute(packed[:, width_x - HALO:, :], 'gx', x_up)  5.33 us
    ppermute x1, starting transfers between devices, with_wide_halo(): east = lax.ppermute(packed[:, :HALO, :], 'gx', x_down)  3.17 us
    eq x48, local copies, waits for them, and re-layouts, resample(): picked = jnp.where(cell_source == member, by_member[member][None], picked)  3.06 us
  transfers between devices with their start and end apart: 5, of which 4 were waited for; matrix products, arithmetic and copies ran while one was open for 8% of the time, Pallas kernels for 0%

profile of v5, /device:TPU:200, one launch (start us, length us, event | category | flops | bytes accessed | tf_op | source)
XLA Modules:
  0.0 87.5 jit_solution(6612408680203844400)
XLA Ops:
  0.0 8.5 %all-to-all-start = ((f32[16,8,8,128]{3,2,1,0:T(8,128)}), f32[16,8,8,128]{3,2,1,0:T(8,128)S(1)}, u32[]{:S(2)}, u32[]{:S(2)}) async-start(f32[16,8,8,128]{3,2,1,0:T(8,128)} %bitcast.87), calls=%async_computation | async-start | bytes 1048576 | tf_op jit(solution)/shard_map/all_to_all | solution.py:166
  8.5 0.8 broadcast_compare_fusion.15
  9.3 0.1 copy.73
  9.4 0.1 copy.74
  9.6 0.1 copy.75
  9.9 0.1 copy.78
  10.2 0.1 copy.81
  11.7 0.1 copy.85
  11.9 0.1 copy.86
  12.1 0.1 copy.87
  12.3 0.1 copy.88
  12.5 11.0 %all-to-all-done = f32[16,8,8,128]{3,2,1,0:T(8,128)S(1)} async-done(((f32[16,8,8,128]{3,2,1,0:T(8,128)}), f32[16,8,8,128]{3,2,1,0:T(8,128)S(1)}, u32[]{:S(2)}, u32[]{:S(2)}) %all-to-all-start) | async-done | bytes 524320 | tf_op jit(solution)/shard_map/all_to_all | solution.py:166
  23.5 1.1 %select_select_fusion = f32[16,8,8,128]{3,2,1,0:T(8,128)S(1)} fusion(f32[8,8,128]{2,1,0:T(8,128)S(1)} %get-tuple-element.10, f32[8,8,128]{2,1,0:T(8,128)S(1)} %get-tuple-element.11, f32[8,8,128]{2,1,0:T(8,128)S(1)} %get-tuple-element.12, f32[8,8,128]{2,1,0:T(8,128)S(1)} %get-tuple-element.13, f32[8,8,128]{2,1,0:T(8,128)S(1)} %get-tuple-element.14, ...), kind=kLoop, calls=%fused_computation.4 | loop fusion | flops 2097152 | bytes 1081344 | tf_op jit(solution)/shard_map/jit(_where)/select_n | solution.py:171
  24.6 19.8 %all_to_all.10 = f32[16,8,8,128]{3,2,1,0:T(8,128)S(1)} all-to-all(f32[16,8,8,128]{3,2,1,0:T(8,128)S(1)} %select_select_fusion), channel_id=1, replica_groups=mesh['dom'=16,'gx'=4,'gy'=8] {'dom'}, dimensions={0} | all-to-all | bytes 1048576 | tf_op jit(solution)/shard_map/all_to_all | solution.py:172
  44.5 3.2 %collective-permute-start = (f32[130,4,128]{2,1,0:T(4,128)S(1)}, f32[130,4,128]{2,1,0:T(4,128)S(1)}, u32[]{:S(2)}, u32[]{:S(2)}) collective-permute-start(f32[130,4,128]{2,1,0:T(4,128)S(1)} %get-tuple-element.7), channel_id=1, source_target_pairs={{8,0},{16,8},{24,16},{0,24},{9,1},{17,9},{25,17},{1,25},{10,2},{18... | collective-permute-start | bytes 798728 | tf_op jit(solution)/shard_map/ppermute | solution.py:35
  47.7 1.9 %collective-permute-start.1 = (f32[130,4,128]{2,1,0:T(4,128)S(1)}, f32[130,4,128]{2,1,0:T(4,128)S(1)}, u32[]{:S(2)}, u32[]{:S(2)}) collective-permute-start(f32[130,4,128]{2,1,0:T(4,128)S(1)} %get-tuple-element.8), channel_id=1, source_target_pairs={{0,8},{8,16},{16,24},{24,0},{1,9},{9,17},{17,25},{25,1},{2,10},{10... | collective-permute-start | bytes 798728 | tf_op jit(solution)/shard_map/ppermute | solution.py:34
  49.6 0.5 and_convert_fusion.refs_2_
  50.1 0.6 multiply_add_fusion.refs_1_
  50.7 0.9 %collective-permute-done = f32[130,4,128]{2,1,0:T(4,128)S(1)} collective-permute-done((f32[130,4,128]{2,1,0:T(4,128)S(1)}, f32[130,4,128]{2,1,0:T(4,128)S(1)}, u32[]{:S(2)}, u32[]{:S(2)}) %collective-permute-start) | collective-permute-done | bytes 266272 | tf_op jit(solution)/shard_map/ppermute | solution.py:35
  51.6 5.3 %collective-permute-done.1 = f32[130,4,128]{2,1,0:T(4,128)S(1)} collective-permute-done((f32[130,4,128]{2,1,0:T(4,128)S(1)}, f32[130,4,128]{2,1,0:T(4,128)S(1)}, u32[]{:S(2)}, u32[]{:S(2)}) %collective-permute-start.1) | collective-permute-done | bytes 266272 | tf_op jit(solution)/shard_map/ppermute | solution.py:34
  56.9 0.1 pad_maximum_fusion.1
  57.0 0.3 fusion.1
  57.4 0.7 copy.69
  58.1 1.9 %collective-permute-start.2 = (f32[130,16,4]{0,1,2:T(8,128)S(1)}, f32[130,16,4]{0,1,2:T(8,128)S(1)}, u32[]{:S(2)}, u32[]{:S(2)}) collective-permute-start(f32[130,16,4]{0,1,2:T(8,128)S(1)} %copy.69), channel_id=1, source_target_pairs={{1,0},{2,1},{3,2},{4,3},{5,4},{6,5},{7,6},{9,8},{10,9},{11,10},{12... | collective-permute-start | bytes 99848 | tf_op jit(solution)/shard_map/ppermute | solution.py:40
  60.0 0.7 copy.70
  60.7 5.5 %collective-permute-start.3 = (f32[130,16,4]{0,1,2:T(8,128)S(1)}, f32[130,16,4]{0,1,2:T(8,128)S(1)}, u32[]{:S(2)}, u32[]{:S(2)}) collective-permute-start(f32[130,16,4]{0,1,2:T(8,128)S(1)} %copy.70), channel_id=1, source_target_pairs={{0,1},{1,2},{2,3},{3,4},{4,5},{5,6},{6,7},{8,9},{9,10},{10,11},{11... | collective-permute-start | bytes 99848 | tf_op jit(solution)/shard_map/ppermute | solution.py:39
  66.2 0.6 pad_maximum_fusion.3.refs_0_
  66.9 0.8 copy.71
  67.6 0.4 collective-permute-done.3
  68.1 0.8 copy.72
  68.9 1.8 %pad_maximum_fusion.refs_3_ = f32[130,16,256]{2,1,0:T(8,128)} fusion(f32[130,16,4]{2,1,0:T(8,128)S(1)} %copy.72, f32[130,16,4]{2,1,0:T(8,128)S(1)} %copy.71, f32[130,4,128]{2,1,0:T(4,128)S(1)} %collective-permute-done.1, f32[130,4,128]{2,1,0:T(4,128)S(1)} %collective-permute-done, f32[2,8,128]{2,1,0:T(8,128)S(1)} %bitcast.90, f32[128,8,128]{2,1,0:T(8,128)S(1)} %bitcast.86, ...), kind=kLoop, calls=%fused_computation | loop fusion | flops 3194880 | bytes 3262464 | tf_op jit(solution)/shard_map/concatenate | solution.py:42
  70.6 16.9 %shard_map.46 = f32[128,8,128]{2,1,0:T(8,128)} custom-call(f32[33]{0:T(128)} %pad_maximum_fusion.3.refs_0_, f32[1,256]{1,0:T(1,128)} %multiply_add_fusion.refs_1_, f32[1,256]{1,0:T(1,128)} %and_convert_fusion.refs_2_, f32[130,16,256]{2,1,0:T(8,128)} %pad_maximum_fusion.refs_3_), custom_call_target="tpu_custom_call" | custom-call | flops 83886080 | bytes 2654208 | tf_op jit(solution)/shard_map/pallas_call | solution.py:143
  (48 shorter events, 2.4 us)
Async XLA Ops:
  0.0 23.5 %all-to-all-start = ((f32[16,8,8,128]{3,2,1,0:T(8,128)}), f32[16,8,8,128]{3,2,1,0:T(8,128)S(1)}, u32[]{:S(2)}, u32[]{:S(2)}) async-start(f32[16,8,8,128]{3,2,1,0:T(8,128)} %bitcast.87), calls=%async_computation | async-start | bytes 1048576 | tf_op jit(solution)/shard_map/all_to_all | solution.py:166
  23.5 20.9 %copy-start = (f32[1,2,8,128]{3,2,1,0:T(8,128)S(1)}, f32[1,2,8,128]{3,2,1,0:T(8,128)}, u32[]{:S(2)}) copy-start(f32[1,2,8,128]{3,2,1,0:T(8,128)} %param.6) | copy-start | bytes 24580
  44.5 7.1 %collective-permute-start = (f32[130,4,128]{2,1,0:T(4,128)S(1)}, f32[130,4,128]{2,1,0:T(4,128)S(1)}, u32[]{:S(2)}, u32[]{:S(2)}) collective-permute-start(f32[130,4,128]{2,1,0:T(4,128)S(1)} %get-tuple-element.7), channel_id=1, source_target_pairs={{8,0},{16,8},{24,16},{0,24},{9,1},{17,9},{25,17},{1,25},{10,2},{18... | collective-permute-start | bytes 798728 | tf_op jit(solution)/shard_map/ppermute | solution.py:35
  47.7 9.2 %collective-permute-start.1 = (f32[130,4,128]{2,1,0:T(4,128)S(1)}, f32[130,4,128]{2,1,0:T(4,128)S(1)}, u32[]{:S(2)}, u32[]{:S(2)}) collective-permute-start(f32[130,4,128]{2,1,0:T(4,128)S(1)} %get-tuple-element.8), channel_id=1, source_target_pairs={{0,8},{8,16},{16,24},{24,0},{1,9},{9,17},{17,25},{25,1},{2,10},{10... | collective-permute-start | bytes 798728 | tf_op jit(solution)/shard_map/ppermute | solution.py:34
  57.4 8.8 %copy-start.1 = (f32[31]{0:T(128)S(1)}, f32[31]{0:T(128)}, u32[]{:S(2)}) copy-start(f32[31]{0:T(128)} %param.7) | copy-start | bytes 376
  58.1 8.8 %collective-permute-start.2 = (f32[130,16,4]{0,1,2:T(8,128)S(1)}, f32[130,16,4]{0,1,2:T(8,128)S(1)}, u32[]{:S(2)}, u32[]{:S(2)}) collective-permute-start(f32[130,16,4]{0,1,2:T(8,128)S(1)} %copy.69), channel_id=1, source_target_pairs={{1,0},{2,1},{3,2},{4,3},{5,4},{6,5},{7,6},{9,8},{10,9},{11,10},{12... | collective-permute-start | bytes 99848 | tf_op jit(solution)/shard_map/ppermute | solution.py:40
  60.7 7.4 %collective-permute-start.3 = (f32[130,16,4]{0,1,2:T(8,128)S(1)}, f32[130,16,4]{0,1,2:T(8,128)S(1)}, u32[]{:S(2)}, u32[]{:S(2)}) collective-permute-start(f32[130,16,4]{0,1,2:T(8,128)S(1)} %copy.70), channel_id=1, source_target_pairs={{0,1},{1,2},{2,3},{3,4},{4,5},{5,6},{6,7},{8,9},{9,10},{10,11},{11... | collective-permute-start | bytes 99848 | tf_op jit(solution)/shard_map/ppermute | solution.py:39

commit v6 on v5

--- a/solution.py
+++ b/solution.py
@@ -101,7 +101,7 @@
                 dst[f * levels + k] = jnp.where(inside, new[f], 0.0)
             return total
 
-        lax.fori_loop(0, levels, level, jnp.zeros((n_rows, lanes), jnp.float32))
+        lax.fori_loop(0, levels, level, jnp.zeros((n_rows, lanes), jnp.float32), unroll=True)
 
     def last_step(src):
         def pieces(i):
@@ -127,7 +127,7 @@
             return totals
 
         zero = jnp.zeros((wx, wy), jnp.float32)
-        lax.fori_loop(0, levels, level, (zero, zero, zero))
+        lax.fori_loop(0, levels, level, (zero, zero, zero), unroll=True)
 
     one_step(full_ref, buf1)
     one_step(buf1, buf0)

time: 87.9 us -> 80.2 us (0.912)
  Pallas kernels: 16.9 us -> 9.17 us
    pallas_call x1, Pallas kernels: 16.9 us -> 9.17 us  [forecast(): pl.pallas_call(kernel, out_shape=jax.ShapeDtypeStruct((state_rows, width_...]
  transfers between devices with their start and end apart: 5 -> 5, of which waited for: 4 -> 4; matrix products, arithmetic and copies ran while one was open for 8% -> 9% of each run, Pallas kernels for 0% -> 0%
where the time goes in v6:
time: 80.2 us; the launch traced here: 79.8 us
  starting transfers between devices  21.2 us (26%)
  blocking collectives  19.8 us (25%)
  waiting for transfers between devices  17.4 us (22%)
  Pallas kernels  9.17 us (11%)
  local copies, waits for them, and re-layouts  6.45 us (8%)
  other arithmetic  5.59 us (7%)
    all_to_all x1, blocking collectives, resample(): back = lax.all_to_all(picked, 'dom', 0, 0, tiled=True)  19.8 us
    all_to_all x1, waiting for transfers between devices, resample(): by_member = lax.all_to_all(parts, 'dom', 0, 0, tiled=True)  11 us
    pallas_call x1, Pallas kernels, forecast(): pl.pallas_call(kernel, out_shape=jax.ShapeDtypeStruct((state_rows, width_...  9.17 us
    all_to_all x1, starting transfers between devices, resample(): by_member = lax.all_to_all(parts, 'dom', 0, 0, tiled=True)  8.49 us
    ppermute x1, starting transfers between devices, with_wide_halo(): south = lax.ppermute(rows[:, :, width_y - HALO:], 'gy', y_up)  5.67 us
    ppermute x1, waiting for transfers between devices, with_wide_halo(): west = lax.ppermute(packed[:, width_x - HALO:, :], 'gx', x_up)  5.33 us
    ppermute x1, starting transfers between devices, with_wide_halo(): east = lax.ppermute(packed[:, :HALO, :], 'gx', x_down)  3.17 us
    eq x48, local copies, waits for them, and re-layouts, resample(): picked = jnp.where(cell_source == member, by_member[member][None], picked)  3.06 us
  transfers between devices with their start and end apart: 5, of which 4 were waited for; matrix products, arithmetic and copies ran while one was open for 9% of the time, Pallas kernels for 0%

profile of v6, /device:TPU:200, one launch (start us, length us, event | category | flops | bytes accessed | tf_op | source)
XLA Modules:
  0.0 79.8 jit_solution(6724709455763633389)
XLA Ops:
  0.0 8.5 %all-to-all-start = ((f32[16,8,8,128]{3,2,1,0:T(8,128)}), f32[16,8,8,128]{3,2,1,0:T(8,128)S(1)}, u32[]{:S(2)}, u32[]{:S(2)}) async-start(f32[16,8,8,128]{3,2,1,0:T(8,128)} %bitcast.87), calls=%async_computation | async-start | bytes 1048576 | tf_op jit(solution)/shard_map/all_to_all | solution.py:166
  8.5 0.8 %broadcast_compare_fusion.15 = (pred[16,1,16]{2,1,0:T(4,128)(4,1)S(1)}, pred[16,1,16]{2,1,0:T(4,128)(4,1)S(1)}, pred[16,1,16]{2,1,0:T(4,128)(4,1)S(1)}, pred[16,...) fusion(s32[16,1,16]{2,1,0:T(1,128)} %param.5), kind=kLoop, calls=%fused_computation.55 | loop fusion | flops 4096 | bytes 5120 | tf_op jit(solution)/shard_map/eq | solution.py:171
  9.3 0.1 copy.73
  9.4 0.1 copy.74
  9.6 0.1 copy.75
  9.9 0.1 copy.78
  10.3 0.1 copy.82
  11.7 0.1 copy.85
  11.9 0.1 copy.86
  12.1 0.1 copy.87
  12.3 0.1 copy.88
  12.5 11.0 %all-to-all-done = f32[16,8,8,128]{3,2,1,0:T(8,128)S(1)} async-done(((f32[16,8,8,128]{3,2,1,0:T(8,128)}), f32[16,8,8,128]{3,2,1,0:T(8,128)S(1)}, u32[]{:S(2)}, u32[]{:S(2)}) %all-to-all-start) | async-done | bytes 524320 | tf_op jit(solution)/shard_map/all_to_all | solution.py:166
  23.5 1.1 %select_select_fusion = f32[16,8,8,128]{3,2,1,0:T(8,128)S(1)} fusion(f32[8,8,128]{2,1,0:T(8,128)S(1)} %get-tuple-element.10, f32[8,8,128]{2,1,0:T(8,128)S(1)} %get-tuple-element.11, f32[8,8,128]{2,1,0:T(8,128)S(1)} %get-tuple-element.12, f32[8,8,128]{2,1,0:T(8,128)S(1)} %get-tuple-element.13, f32[8,8,128]{2,1,0:T(8,128)S(1)} %get-tuple-element.14, ...), kind=kLoop, calls=%fused_computation.4 | loop fusion | flops 2097152 | bytes 1081344 | tf_op jit(solution)/shard_map/jit(_where)/select_n | solution.py:171
  24.6 19.8 %all_to_all.10 = f32[16,8,8,128]{3,2,1,0:T(8,128)S(1)} all-to-all(f32[16,8,8,128]{3,2,1,0:T(8,128)S(1)} %select_select_fusion), channel_id=1, replica_groups=mesh['dom'=16,'gx'=4,'gy'=8] {'dom'}, dimensions={0} | all-to-all | bytes 1048576 | tf_op jit(solution)/shard_map/all_to_all | solution.py:172
  44.5 3.2 %collective-permute-start = (f32[130,4,128]{2,1,0:T(4,128)S(1)}, f32[130,4,128]{2,1,0:T(4,128)S(1)}, u32[]{:S(2)}, u32[]{:S(2)}) collective-permute-start(f32[130,4,128]{2,1,0:T(4,128)S(1)} %get-tuple-element.7), channel_id=1, source_target_pairs={{8,0},{16,8},{24,16},{0,24},{9,1},{17,9},{25,17},{1,25},{10,2},{18... | collective-permute-start | bytes 798728 | tf_op jit(solution)/shard_map/ppermute | solution.py:35
  47.7 1.9 %collective-permute-start.1 = (f32[130,4,128]{2,1,0:T(4,128)S(1)}, f32[130,4,128]{2,1,0:T(4,128)S(1)}, u32[]{:S(2)}, u32[]{:S(2)}) collective-permute-start(f32[130,4,128]{2,1,0:T(4,128)S(1)} %get-tuple-element.8), channel_id=1, source_target_pairs={{0,8},{8,16},{16,24},{24,0},{1,9},{9,17},{17,25},{25,1},{2,10},{10... | collective-permute-start | bytes 798728 | tf_op jit(solution)/shard_map/ppermute | solution.py:34
  49.6 0.5 and_convert_fusion.refs_2_
  50.1 0.6 multiply_add_fusion.refs_1_
  50.7 0.9 %collective-permute-done = f32[130,4,128]{2,1,0:T(4,128)S(1)} collective-permute-done((f32[130,4,128]{2,1,0:T(4,128)S(1)}, f32[130,4,128]{2,1,0:T(4,128)S(1)}, u32[]{:S(2)}, u32[]{:S(2)}) %collective-permute-start) | collective-permute-done | bytes 266272 | tf_op jit(solution)/shard_map/ppermute | solution.py:35
  51.6 5.3 %collective-permute-done.1 = f32[130,4,128]{2,1,0:T(4,128)S(1)} collective-permute-done((f32[130,4,128]{2,1,0:T(4,128)S(1)}, f32[130,4,128]{2,1,0:T(4,128)S(1)}, u32[]{:S(2)}, u32[]{:S(2)}) %collective-permute-start.1) | collective-permute-done | bytes 266272 | tf_op jit(solution)/shard_map/ppermute | solution.py:34
  56.9 0.1 pad_maximum_fusion.1
  57.0 0.3 fusion.1
  57.4 0.7 copy.69
  58.1 1.9 %collective-permute-start.2 = (f32[130,16,4]{0,1,2:T(8,128)S(1)}, f32[130,16,4]{0,1,2:T(8,128)S(1)}, u32[]{:S(2)}, u32[]{:S(2)}) collective-permute-start(f32[130,16,4]{0,1,2:T(8,128)S(1)} %copy.69), channel_id=1, source_target_pairs={{1,0},{2,1},{3,2},{4,3},{5,4},{6,5},{7,6},{9,8},{10,9},{11,10},{12... | collective-permute-start | bytes 99848 | tf_op jit(solution)/shard_map/ppermute | solution.py:40
  60.0 0.7 copy.70
  60.7 5.7 %collective-permute-start.3 = (f32[130,16,4]{0,1,2:T(8,128)S(1)}, f32[130,16,4]{0,1,2:T(8,128)S(1)}, u32[]{:S(2)}, u32[]{:S(2)}) collective-permute-start(f32[130,16,4]{0,1,2:T(8,128)S(1)} %copy.70), channel_id=1, source_target_pairs={{0,1},{1,2},{2,3},{3,4},{4,5},{5,6},{6,7},{8,9},{9,10},{10,11},{11... | collective-permute-start | bytes 99848 | tf_op jit(solution)/shard_map/ppermute | solution.py:39
  66.4 0.6 pad_maximum_fusion.3.refs_0_
  67.0 0.8 copy.71
  67.8 0.2 collective-permute-done.3
  68.1 0.8 copy.72
  68.9 1.8 %pad_maximum_fusion.refs_3_ = f32[130,16,256]{2,1,0:T(8,128)} fusion(f32[130,16,4]{2,1,0:T(8,128)S(1)} %copy.72, f32[130,16,4]{2,1,0:T(8,128)S(1)} %copy.71, f32[130,4,128]{2,1,0:T(4,128)S(1)} %collective-permute-done.1, f32[130,4,128]{2,1,0:T(4,128)S(1)} %collective-permute-done, f32[2,8,128]{2,1,0:T(8,128)S(1)} %bitcast.90, f32[128,8,128]{2,1,0:T(8,128)S(1)} %bitcast.86, ...), kind=kLoop, calls=%fused_computation | loop fusion | flops 3194880 | bytes 3262464 | tf_op jit(solution)/shard_map/concatenate | solution.py:42
  70.6 9.2 %shard_map.46 = f32[128,8,128]{2,1,0:T(8,128)} custom-call(f32[33]{0:T(128)} %pad_maximum_fusion.3.refs_0_, f32[1,256]{1,0:T(1,128)} %multiply_add_fusion.refs_1_, f32[1,256]{1,0:T(1,128)} %and_convert_fusion.refs_2_, f32[130,16,256]{2,1,0:T(8,128)} %pad_maximum_fusion.refs_3_), custom_call_target="tpu_custom_call" | custom-call | flops 83886080 | bytes 2654208 | tf_op jit(solution)/shard_map/pallas_call | solution.py:143
  (48 shorter events, 2.4 us)
Async XLA Ops:
  0.0 23.5 %all-to-all-start = ((f32[16,8,8,128]{3,2,1,0:T(8,128)}), f32[16,8,8,128]{3,2,1,0:T(8,128)S(1)}, u32[]{:S(2)}, u32[]{:S(2)}) async-start(f32[16,8,8,128]{3,2,1,0:T(8,128)} %bitcast.87), calls=%async_computation | async-start | bytes 1048576 | tf_op jit(solution)/shard_map/all_to_all | solution.py:166
  23.5 20.9 %copy-start = (f32[1,2,8,128]{3,2,1,0:T(8,128)S(1)}, f32[1,2,8,128]{3,2,1,0:T(8,128)}, u32[]{:S(2)}) copy-start(f32[1,2,8,128]{3,2,1,0:T(8,128)} %param.6) | copy-start | bytes 24580
  44.5 7.1 %collective-permute-start = (f32[130,4,128]{2,1,0:T(4,128)S(1)}, f32[130,4,128]{2,1,0:T(4,128)S(1)}, u32[]{:S(2)}, u32[]{:S(2)}) collective-permute-start(f32[130,4,128]{2,1,0:T(4,128)S(1)} %get-tuple-element.7), channel_id=1, source_target_pairs={{8,0},{16,8},{24,16},{0,24},{9,1},{17,9},{25,17},{1,25},{10,2},{18... | collective-permute-start | bytes 798728 | tf_op jit(solution)/shard_map/ppermute | solution.py:35
  47.7 9.2 %collective-permute-start.1 = (f32[130,4,128]{2,1,0:T(4,128)S(1)}, f32[130,4,128]{2,1,0:T(4,128)S(1)}, u32[]{:S(2)}, u32[]{:S(2)}) collective-permute-start(f32[130,4,128]{2,1,0:T(4,128)S(1)} %get-tuple-element.8), channel_id=1, source_target_pairs={{0,8},{8,16},{16,24},{24,0},{1,9},{9,17},{17,25},{25,1},{2,10},{10... | collective-permute-start | bytes 798728 | tf_op jit(solution)/shard_map/ppermute | solution.py:34
  57.4 9.0 %copy-start.1 = (f32[31]{0:T(128)S(1)}, f32[31]{0:T(128)}, u32[]{:S(2)}) copy-start(f32[31]{0:T(128)} %param.7) | copy-start | bytes 376
  58.1 9.0 %collective-permute-start.2 = (f32[130,16,4]{0,1,2:T(8,128)S(1)}, f32[130,16,4]{0,1,2:T(8,128)S(1)}, u32[]{:S(2)}, u32[]{:S(2)}) collective-permute-start(f32[130,16,4]{0,1,2:T(8,128)S(1)} %copy.69), channel_id=1, source_target_pairs={{1,0},{2,1},{3,2},{4,3},{5,4},{6,5},{7,6},{9,8},{10,9},{11,10},{12... | collective-permute-start | bytes 99848 | tf_op jit(solution)/shard_map/ppermute | solution.py:40
  60.7 7.4 %collective-permute-start.3 = (f32[130,16,4]{0,1,2:T(8,128)S(1)}, f32[130,16,4]{0,1,2:T(8,128)S(1)}, u32[]{:S(2)}, u32[]{:S(2)}) collective-permute-start(f32[130,16,4]{0,1,2:T(8,128)S(1)} %copy.70), channel_id=1, source_target_pairs={{0,1},{1,2},{2,3},{3,4},{4,5},{5,6},{6,7},{8,9},{9,10},{10,11},{11... | collective-permute-start | bytes 99848 | tf_op jit(solution)/shard_map/ppermute | solution.py:39
